TPU v7x, 512 devices: a whole 4x4x16 slice. The times are simulated.
512 devices in a mesh: dp: 16 (over z_lo, x), ctx: 32 (over y, z_hi, core).
Axes of the slice: x: 4, y: 4, z: 16 (z_hi: 4, z_lo: 4; z = z_hi * 4 + z_lo), core: 2. Of those that a mesh axis runs over, the one named last changes fastest.
Arguments:
- tokens: bfloat16 [16, 4096, 4096], P('dp', 'ctx'), may hold values from -6 to 6
- grad_attn: bfloat16 [16, 4096, 1024], P('dp', 'ctx'), may hold values from -6 to 6
- w_packed: bfloat16 [10240, 128], P('ctx'), may hold values from -0.1875 to 0.1875
- block_rows: int32 [10, 8], replicated, may hold values from 0 to 31, as said below
- span_pairs: int32 [32, 2], replicated, may hold values from 0 to 63, as said below
Outputs:
- grad_tokens: bfloat16 [16, 4096, 4096], P('dp', 'ctx')
- grad_weights: float32 [10240, 128], P('ctx')
Inputs may be any that keep to these rules, and one draw needn't show every extreme that they name: `block_rows`: row c lists the 8 row blocks in which column block c is nonzero, all different; rows 0 to 3 together list each of the 32 row blocks exactly once. Index k of ctx holds spans span_pairs[k, 0] and span_pairs[k, 1] = 63 - span_pairs[k, 0]; the first column takes each of 0 to 31 once.
All inputs are finite; a program needn't handle non-finite values.
Results may differ from a plain program's by a relative error of at most 0.0087.
Values may be sent and summed in bfloat16 or wider, within the bound.
A program may use at most 64 MiB of HBM per device.

v0:
```python
import math

import jax
import jax.numpy as jnp
from jax import lax
from jax.sharding import PartitionSpec as P

D = 4096
HD = 128
BLK = 128
QPG = 8
GROUPS = 1
SPAN = 64
NRB = 32
NBR = 8
NCB = 10
NNZ = 80


EPSILON = 1e-06


def norm_forward(values):
    factor = lax.rsqrt(jnp.mean(values * values, axis=-1, keepdims=True) + EPSILON)
    return (values * factor, factor)


def norm_backward(values, factor, upstream):
    return factor * upstream - values * (factor * factor * factor) * jnp.mean(
        upstream * values, axis=-1, keepdims=True
    )


def span_part(array, which):
    return array[which * SPAN : (which + 1) * SPAN]


def positions_of(span_ids):
    return (span_ids[:, None] * SPAN + jnp.arange(SPAN, dtype=jnp.int32)[None, :]).reshape(-1)


def masked_scores(query_part, query_pos, key_part, key_pos):
    raw_scores = jnp.einsum(
        "tgqd,ugd->tgqu", query_part, key_part, preferred_element_type=jnp.float32
    ) / math.sqrt(HD)
    keep = key_pos[None, None, None, :] <= query_pos[:, None, None, None]
    return jnp.where(keep, jnp.exp(raw_scores), 0.0)


def forward_tile(query_part, query_pos, key_part, value_part, key_pos):
    exp_scores = masked_scores(query_part, query_pos, key_part, key_pos)
    weighted = jnp.einsum(
        "tgqu,ugd->tgqd",
        exp_scores.astype(jnp.bfloat16),
        value_part,
        preferred_element_type=jnp.float32,
    )
    return (jnp.sum(exp_scores, axis=-1), weighted)


def backward_tile(
    query_part, upstream_part, total_part, delta_part, query_pos, key_part, value_part, key_pos
):
    exp_scores = masked_scores(query_part, query_pos, key_part, key_pos)
    prob = exp_scores / total_part[..., None]
    dprob = jnp.einsum(
        "tgqd,ugd->tgqu", upstream_part, value_part, preferred_element_type=jnp.float32
    )
    dscore = (prob * (dprob - delta_part[..., None]) / math.sqrt(HD)).astype(jnp.bfloat16)
    part_query = jnp.einsum("tgqu,ugd->tgqd", dscore, key_part, preferred_element_type=jnp.float32)
    part_key = jnp.einsum("tgqu,tgqd->ugd", dscore, query_part, preferred_element_type=jnp.float32)
    part_value = jnp.einsum(
        "tgqu,tgqd->ugd",
        prob.astype(jnp.bfloat16),
        upstream_part,
        preferred_element_type=jnp.float32,
    )
    return (part_query, part_key, part_value)


def empty_forward():
    return (
        jnp.zeros((SPAN, GROUPS, QPG), jnp.float32),
        jnp.zeros((SPAN, GROUPS, QPG, HD), jnp.float32),
    )


def per_device(tokens, grad_attn, w_packed, block_rows, span_pairs):
    ndevices = lax.axis_size("ctx")
    my_index = lax.axis_index("ctx")
    tok_count = tokens.shape[1]
    nquery = GROUPS * QPG
    weights = lax.all_gather(w_packed, "ctx", axis=0, tiled=True).reshape(NCB, NBR, BLK, BLK)
    flat_ids = block_rows.reshape(-1)
    selected = jnp.take(tokens[0].reshape(tok_count, NRB, BLK), flat_ids, axis=1).reshape(
        tok_count, NCB, NBR, BLK
    )
    projected = jnp.einsum(
        "tcri,crio->tco", selected, weights, preferred_element_type=jnp.float32
    ).astype(jnp.bfloat16)
    query_raw = projected[:, :nquery].astype(jnp.float32).reshape(tok_count, GROUPS, QPG, HD)
    key_raw = projected[:, nquery : nquery + GROUPS].astype(jnp.float32)
    values = projected[:, nquery + GROUPS :]
    query_norm, query_factor = norm_forward(query_raw)
    key_norm, key_factor = norm_forward(key_raw)
    query_hat = query_norm.astype(jnp.bfloat16)
    key_hat = key_norm.astype(jnp.bfloat16)
    upstream = grad_attn[0].reshape(tok_count, GROUPS, QPG, HD)
    my_pair = span_pairs[my_index]
    query_pos = positions_of(my_pair)
    zero_rows, zero_out = empty_forward()
    gathered_keys, gathered_values = (
        lax.all_gather(key_hat, "ctx", axis=0, tiled=True),
        lax.all_gather(values, "ctx", axis=0, tiled=True),
    )
    all_positions = positions_of(span_pairs.reshape(-1))
    length = all_positions.shape[0]
    inverse = (
        jnp.zeros((length,), jnp.int32).at[all_positions].set(jnp.arange(length, dtype=jnp.int32))
    )
    sorted_keys = jnp.take(gathered_keys, inverse, axis=0)
    sorted_values = jnp.take(gathered_values, inverse, axis=0)
    key_block = math.gcd(512, length)
    total_parts = []
    weighted_parts = []
    for row_part in range(2):
        query_part = span_part(query_hat, row_part)
        pos_part = span_part(query_pos, row_part)
        block_count = ((my_pair[row_part] + 1) * SPAN + key_block - 1) // key_block

        def forward_loop(block_index, loop_state):
            first_row = block_index * key_block
            key_piece = lax.dynamic_slice_in_dim(sorted_keys, first_row, key_block, 0)
            value_piece = lax.dynamic_slice_in_dim(sorted_values, first_row, key_block, 0)
            key_pos = first_row + jnp.arange(key_block, dtype=jnp.int32)
            part_total, part_weighted = forward_tile(
                query_part, pos_part, key_piece, value_piece, key_pos
            )
            return (loop_state[0] + part_total, loop_state[1] + part_weighted)

        total_part, weighted_part = lax.fori_loop(
            0, block_count, forward_loop, (zero_rows, zero_out)
        )
        total_parts.append(total_part)
        weighted_parts.append(weighted_part)
    totals = jnp.concatenate(total_parts, axis=0)
    weighted = jnp.concatenate(weighted_parts, axis=0)
    attn_out = weighted / totals[..., None]
    deltas = jnp.sum(upstream.astype(jnp.float32) * attn_out, axis=-1)
    grad_keys_all = jnp.zeros((length, GROUPS, HD), jnp.float32)
    grad_values_all = jnp.zeros((length, GROUPS, HD), jnp.float32)
    query_parts = []
    for row_part in range(2):
        query_part = span_part(query_hat, row_part)
        upstream_part = span_part(upstream, row_part)
        total_part = span_part(totals, row_part)
        delta_part = span_part(deltas, row_part)
        pos_part = span_part(query_pos, row_part)
        block_count = ((my_pair[row_part] + 1) * SPAN + key_block - 1) // key_block

        def backward_loop(block_index, loop_state):
            grad_part, keys_acc, values_acc = loop_state
            first_row = block_index * key_block
            key_piece = lax.dynamic_slice_in_dim(sorted_keys, first_row, key_block, 0)
            value_piece = lax.dynamic_slice_in_dim(sorted_values, first_row, key_block, 0)
            key_pos = first_row + jnp.arange(key_block, dtype=jnp.int32)
            part_query, part_key, part_value = backward_tile(
                query_part,
                upstream_part,
                total_part,
                delta_part,
                pos_part,
                key_piece,
                value_piece,
                key_pos,
            )
            keys_acc = lax.dynamic_update_slice_in_dim(
                keys_acc,
                lax.dynamic_slice_in_dim(keys_acc, first_row, key_block, 0) + part_key,
                first_row,
                0,
            )
            values_acc = lax.dynamic_update_slice_in_dim(
                values_acc,
                lax.dynamic_slice_in_dim(values_acc, first_row, key_block, 0) + part_value,
                first_row,
                0,
            )
            return (grad_part + part_query, keys_acc, values_acc)

        grad_part, grad_keys_all, grad_values_all = lax.fori_loop(
            0, block_count, backward_loop, (zero_out, grad_keys_all, grad_values_all)
        )
        query_parts.append(grad_part)
    grad_query_hat = jnp.concatenate(query_parts, axis=0)
    owner_keys = jnp.take(grad_keys_all, all_positions, axis=0)
    owner_values = jnp.take(grad_values_all, all_positions, axis=0)
    grad_key_hat, grad_value = (
        lax.psum_scatter(owner_keys, "ctx", scatter_dimension=0, tiled=True),
        lax.psum_scatter(owner_values, "ctx", scatter_dimension=0, tiled=True),
    )
    grad_query = norm_backward(query_raw, query_factor, grad_query_hat).astype(jnp.bfloat16)
    grad_key = norm_backward(key_raw, key_factor, grad_key_hat).astype(jnp.bfloat16)
    grad_proj = jnp.concatenate(
        [grad_query.reshape(tok_count, nquery, HD), grad_key, grad_value.astype(jnp.bfloat16)],
        axis=1,
    )
    partial_w = jnp.einsum(
        "tcri,tco->crio", selected, grad_proj, preferred_element_type=jnp.float32
    ).astype(jnp.bfloat16)
    partial_w = partial_w.reshape(ndevices, NNZ * BLK // ndevices, BLK)
    received = lax.all_to_all(partial_w, "ctx", split_axis=0, concat_axis=0, tiled=True)
    summed = jnp.sum(received.astype(jnp.float32), axis=0)
    grad_weights = lax.psum(summed, "dp")
    placement = (block_rows[:, :, None] == jnp.arange(NRB, dtype=jnp.int32)[None, None, :]).astype(
        jnp.bfloat16
    )
    dense_weights = jnp.einsum(
        "crb,crio->cbio", placement, weights, preferred_element_type=jnp.float32
    ).astype(jnp.bfloat16)
    grad_tokens = jnp.einsum(
        "tco,cbio->tbi", grad_proj, dense_weights, preferred_element_type=jnp.float32
    )
    grad_tokens = grad_tokens.reshape(1, tok_count, D).astype(jnp.bfloat16)
    return (grad_tokens, grad_weights)


def solution(mesh):
    in_specs = (P("dp", "ctx", None), P("dp", "ctx", None), P("ctx", None), P(), P())
    out_specs = (P("dp", "ctx", None), P("ctx", None))
    return jax.shard_map(
        per_device, mesh=mesh, in_specs=in_specs, out_specs=out_specs, check_vma=False
    )
```

profile of v0, /device:TPU:24, one launch (start us, length us, event | category | flops | bytes accessed | tf_op | source)
XLA Modules:
  0.0 899.6 jit_solution(7687914851189852073)
XLA Ops:
  8.8 1.6 copy.27
  11.1 2.5 gather_fusion
  13.7 3.3 copy.30
  17.1 80.8 %all-gather.4.cloned.1.call-done = bf16[10240,128]{1,0:T(8,128)(2,1)} async-done(((bf16[320,128]{1,0:T(8,128)(2,1)}), bf16[10240,128]{1,0:T(8,128)(2,1)}) %all-gather.4.cloned.1.call-update) | async-done | bytes 2621456 | tf_op jit(solution)/shard_map/all_gather | solution.py:93
  97.9 2.9 fusion.98
  106.0 15.5 %scatter_custom_fusion = s32[4096]{0:T(1024)S(1)} fusion(s32[4096]{0:T(1024)S(1)} %bitcast.446, s32[4096]{0:T(1024)S(1)} %iota.33, s32[]{:T(128)} %constant.141.clone.1), kind=kCustom, calls=%fused_computation.178 | custom fusion | bytes 16388 | tf_op jit(solution)/shard_map/scatter | solution.py:119
  122.0 45.3 %all-gather.6.cloned.1.call-done = bf16[4096,1,128]{2,0,1:T(8,128)(2,1)} async-done(((bf16[128,1,128]{2,0,1:T(8,128)(2,1)}), bf16[4096,1,128]{2,0,1:T(8,128)(2,1)}) %all-gather.6.cloned.1.call-update) | async-done | bytes 1048592 | tf_op jit(solution)/shard_map/all_gather | solution.py:113
  167.4 15.6 %gather_fusion.1 = bf16[4096,128]{1,0:T(8,128)(2,1)} fusion(bf16[4096,128]{1,0:T(8,128)(2,1)} %bitcast.427, s32[4096]{0:T(1024)S(1)} %fusion.118), kind=kCustom, calls=%fused_computation.clone | custom fusion | bytes 2113536 | tf_op jit(solution)/shard_map/jit(_take)/gather | solution.py:121
  182.9 53.6 %all-gather.8.cloned.1.call-done = bf16[4096,1,128]{2,0,1:T(8,128)(2,1)} async-done(((bf16[128,1,128]{2,0,1:T(8,128)(2,1)}), bf16[4096,1,128]{2,0,1:T(8,128)(2,1)}) %all-gather.8.cloned.1.call-update) | async-done | bytes 1048592 | tf_op jit(solution)/shard_map/all_gather | solution.py:114
  236.5 15.7 %gather_fusion.2 = bf16[4096,128]{1,0:T(8,128)(2,1)} fusion(bf16[4096,128]{1,0:T(8,128)(2,1)} %bitcast.428, s32[4096]{0:T(1024)S(1)} %fusion.118), kind=kCustom, calls=%fused_computation.2.clone | custom fusion | bytes 2113536 | tf_op jit(solution)/shard_map/jit(_take)/gather | solution.py:122
  252.2 3.6 bitcast_select_fusion.2
  255.8 6.5 while.53
  262.4 1.9 while.52
  266.6 1.5 fusion.106
  268.2 1.5 broadcast.342
  269.8 12.5 %while.54 = (s32[]{:T(128)}, f32[64,1,8,128]{3,0,2,1:T(8,128)S(1)}, f32[4096,1,128]{2,0,1:T(8,128)}, f32[4096,1,128]{2,0,1:T(8,128)S(1)}, s32[]{:T(128)}, /*inde...) while((s32[]{:T(128)}, f32[64,1,8,128]{3,0,2,1:T(8,128)S(1)}, ...), condition=%wide.region_11.13_spmd, body=%wide.region_10.12_spmd.sunk | while | flops 337871360 | bytes 7283163 | solution.py:191
  269.9 1.3 fusion.191
  272.5 2.0 fusion.194
  276.2 1.3 fusion.191
  278.7 2.0 fusion.194
  282.3 43.8 %while.55 = (s32[]{:T(128)}, f32[64,1,8,128]{3,0,2,1:T(8,128)S(1)}, f32[4096,1,128]{2,0,1:T(8,128)}, f32[4096,1,128]{2,0,1:T(8,128)S(1)}, s32[]{:T(128)}, /*inde...) while((s32[]{:T(128)}, f32[64,1,8,128]{3,0,2,1:T(8,128)S(1)}, ...), condition=%wide.region_13.15_spmd, body=%wide.region_12.14_spmd.sunk | while | flops 337871360 | bytes 7283163 | solution.py:191
  282.4 1.3 fusion.206
  285.0 2.0 fusion.209
  288.7 1.3 fusion.206
  291.2 2.0 fusion.209
  294.9 1.3 fusion.206
  297.4 2.0 fusion.209
  301.1 1.3 fusion.206
  303.7 2.0 fusion.209
  307.4 1.3 fusion.206
  309.9 2.0 fusion.209
  313.6 1.3 fusion.206
  316.1 2.0 fusion.209
  319.8 1.3 fusion.206
  322.3 2.0 fusion.209
  326.1 14.1 %gather_fusion.4 = f32[4096,128]{1,0:T(8,128)} fusion(f32[4096,128]{1,0:T(8,128)S(1)} %bitcast.425, s32[4096]{0:T(1024)S(1)} %fusion.119), kind=kCustom, calls=%fused_computation.3.clone | custom fusion | bytes 4210688 | tf_op jit(solution)/shard_map/jit(_take)/gather | solution.py:197
  340.2 15.8 %gather_fusion.3 = f32[4096,128]{1,0:T(8,128)} fusion(f32[4096,128]{1,0:T(8,128)} %bitcast.426, s32[4096]{0:T(1024)S(1)} %fusion.119), kind=kCustom, calls=%fused_computation.1.clone | custom fusion | bytes 4210688 | tf_op jit(solution)/shard_map/jit(_take)/gather | solution.py:196
  356.1 3.5 bitcast_select_fusion.1
  360.9 114.8 %reduce-scatter.3.cloned.1.call-done = f32[128,1,128]{2,0,1:T(8,128)} async-done(((f32[4096,1,128]{2,0,1:T(8,128)}), f32[128,1,128]{2,0,1:T(8,128)}) %reduce-scatter.3.cloned.1.call-update) | async-done | bytes 65552 | tf_op jit(solution)/shard_map/reduce_scatter | solution.py:199
  476.7 120.0 %reduce-scatter.5.cloned.1.call-done = f32[128,1,128]{2,0,1:T(8,128)} async-done(((f32[4096,1,128]{2,0,1:T(8,128)}), f32[128,1,128]{2,0,1:T(8,128)}) %reduce-scatter.5.cloned.1.call-update) | async-done | bytes 65552 | tf_op jit(solution)/shard_map/reduce_scatter | solution.py:200
  598.5 4.1 fusion.91
  602.6 10.0 %all-to-all-start = ((bf16[32,320,128]{2,1,0:T(8,128)(2,1)}), bf16[32,320,128]{2,1,0:T(8,128)(2,1)S(1)}, u32[]{:S(2)}, u32[]{:S(2)}) async-start(bf16[32,320,128]{2,1,0:T(8,128)(2,1)} %bitcast.437), calls=%async_computation.2 | async-start | bytes 5242880 | tf_op jit(solution)/shard_map/all_to_all | solution.py:212
  612.6 7.0 convolution_convert_fusion
  619.5 111.6 %all-to-all-done = bf16[32,320,128]{2,1,0:T(8,128)(2,1)S(1)} async-done(((bf16[32,320,128]{2,1,0:T(8,128)(2,1)}), bf16[32,320,128]{2,1,0:T(8,128)(2,1)S(1)}, u32[]{:S(2)}, u32[]{:S(2)}) %all-to-all-start) | async-done | bytes 2621472 | tf_op jit(solution)/shard_map/all_to_all | solution.py:212
  732.2 12.2 %bitcast_convert_fusion = bf16[128,32,128]{0,2,1:T(8,128)(2,1)S(1)} fusion(bf16[10,32,128,128]{3,1,2,0:T(8,128)(2,1)} %convolution_convert_fusion, bf16[128,1,128]{2,0,1:T(8,128)(2,1)S(1)} %convert_element_type.99, bf16[128,1,128]{2,0,1:T(8,128)(2,1)S(1)} %fusion.113, bf16[128,8,128]{2,0,1:T(8,128)(2,1)S(1)} %fusion.103), kind=kOutput, calls=%fused_computation.124 | convolution fusion | flops 1343684608 | bytes 11862016 | tf_op jit(solution)/shard_map/tco,cbio->tbi/dot_general | solution.py:221
  744.4 1.3 copy.41
  745.7 145.4 %all-reduce.2.cloned.1.call-done = f32[320,128]{1,0:T(8,128)} async-done(((f32[320,128]{1,0:T(8,128)}), f32[320,128]{1,0:T(8,128)}) %all-reduce.2.cloned.1.call-update) | async-done | bytes 163856 | tf_op jit(solution)/shard_map/psum | solution.py:214
  891.1 1.6 copy.102
  (172 shorter events, 48.1 us)
Async XLA Ops:
  7.2 90.7 %all-gather.4.cloned.1.call-start = ((), (), s32[]{:S(2)}) async-start(), calls=%async_computation.3 | async-start | bytes 2703360 | tf_op jit(solution)/shard_map/all_gather | solution.py:93
  7.9 159.5 %all-gather.6.cloned.1.call-start = ((), (), s32[]{:S(2)}) async-start(), calls=%async_computation.4 | async-start | bytes 1081344 | tf_op jit(solution)/shard_map/all_gather | solution.py:113
  13.7 3.3 copy-start.5
  16.9 83.8 %copy-start.3 = (bf16[128,10,8,128]{0,3,2,1:T(8,128)(2,1)}, bf16[128,10,8,128]{0,3,2,1:T(8,128)(2,1)S(1)}, u32[]{:S(2)}) copy-start(bf16[128,10,8,128]{0,3,2,1:T(8,128)(2,1)S(1)} %copy.30) | copy-start | bytes 7864324
  97.9 3.8 copy-start.6
  97.9 4.4 copy-start.4
  101.6 134.9 %all-gather.8.cloned.1.call-start = ((), (), s32[]{:S(2)}) async-start(), calls=%async_computation.5 | async-start | bytes 1081344 | tf_op jit(solution)/shard_map/all_gather | solution.py:114
  103.0 372.8 %reduce-scatter.3.cloned.1.call-start = ((), (), s32[]{:S(2)}) async-start(), calls=%async_computation.6 | async-start | bytes 2162688 | tf_op jit(solution)/shard_map/reduce_scatter | solution.py:199
  264.2 3.9 copy-start
  264.2 3.9 copy-start.2
  340.2 15.8 %copy-start.1 = (f32[4096,128]{1,0:T(8,128)S(1)}, f32[4096,128]{1,0:T(8,128)}, u32[]{:S(2)}) copy-start(f32[4096,128]{1,0:T(8,128)} %gather_fusion.4) | copy-start | bytes 6291460
  359.6 237.0 %reduce-scatter.5.cloned.1.call-start = ((), (), s32[]{:S(2)}) async-start(), calls=%async_computation.7 | async-start | bytes 2162688 | tf_op jit(solution)/shard_map/reduce_scatter | solution.py:200
  602.6 128.6 %all-to-all-start = ((bf16[32,320,128]{2,1,0:T(8,128)(2,1)}), bf16[32,320,128]{2,1,0:T(8,128)(2,1)S(1)}, u32[]{:S(2)}, u32[]{:S(2)}) async-start(bf16[32,320,128]{2,1,0:T(8,128)(2,1)} %bitcast.437), calls=%async_computation.2 | async-start | bytes 5242880 | tf_op jit(solution)/shard_map/all_to_all | solution.py:212
  612.5 278.6 %all-reduce.2.cloned.1.call-start = ((), (), s32[]{:S(2)}) async-start(), calls=%async_computation.8 | async-start | bytes 327680 | tf_op jit(solution)/shard_map/psum | solution.py:214
Sparse Core Ops, SparseCore 0:
  11.1 86.7 all-gather.3
  101.7 65.6 all-gather.5
  171.1 65.3 all-gather.7
  359.8 115.9 reduce-scatter.2
  480.0 116.5 reduce-scatter.4
  732.3 158.7 all-reduce.1
where the time goes:
time: 902 us; the launch traced here: 900 us
  waiting for transfers between devices  673 us (75%)
  local copies, waits for them, and re-layouts  95.3 us (11%)
  matrix products  87.8 us (10%)
  other arithmetic  16.5 us (2%)
  between operations  15.8 us (2%)
  starting transfers between devices  10.2 us (1%)
    psum x1, waiting for transfers between devices, per_device(): grad_weights = lax.psum(summed, 'dp')  145 us
    reduce_scatter x1, waiting for transfers between devices, per_device(): lax.psum_scatter(owner_values, 'ctx', scatter_dimension=0, tiled=True)  120 us
    reduce_scatter x1, waiting for transfers between devices, per_device(): lax.psum_scatter(owner_keys, 'ctx', scatter_dimension=0, tiled=True)  115 us
    all_to_all x1, waiting for transfers between devices, per_device(): lax.all_to_all(partial_w, 'ctx', split_axis=0, concat_axis=0, tiled=True)  112 us
    all_gather x1, waiting for transfers between devices, per_device(): lax.all_gather(w_packed, 'ctx', axis=0, tiled=True)  80.8 us
    all_gather x1, waiting for transfers between devices, per_device(): lax.all_gather(values, 'ctx', axis=0, tiled=True)  53.6 us
    all_gather x1, waiting for transfers between devices, per_device(): lax.all_gather(key_hat, 'ctx', axis=0, tiled=True)  45.3 us
  transfers between devices with their start and end apart: 7, of which 7 were waited for; matrix products, arithmetic and copies ran while one was open for 7% of the time, Pallas kernels for 0%

commit v1 on v0

v1 whole, which is shorter than its diff:
```python
import functools
import math

import jax
import jax.numpy as jnp
from jax import lax
from jax.experimental import pallas as pl
from jax.experimental.pallas import tpu as pltpu
from jax.sharding import PartitionSpec as P

D = 4096
HD = 128
BLK = 128
QPG = 8
SPAN = 64
NRB = 32
NBR = 8
NCB = 10
EPSILON = 1e-06
SCALE = 1.0 / math.sqrt(HD)
SHARD = 320
PIECE = 80
CHUNK = 256
BF = jnp.bfloat16
F32 = jnp.float32
MESH = pl.DeviceIdType.MESH


def place():
    dp = lax.axis_index("dp")
    ctx = lax.axis_index("ctx")
    return dp % 4, dp // 4, ctx // 8, (ctx // 2) % 4, ctx % 2


def peers():
    x, l, y, h, c = place()

    def at(px, plo, py, ph, pc):
        return (plo * 4 + px, py * 8 + ph * 2 + pc)

    return {
        "x": lambda d: at((x + d) % 4, l, y, h, c),
        "l": lambda d: at(x, (l + d) % 4, y, h, c),
        "y": lambda d: at(x, l, (y + d) % 4, h, c),
        "h": lambda d: at(x, l, y, (h + d) % 4, c),
        "c": lambda d: at(x, l, y, h, (c + d) % 2),
    }


def remote(src, dst, send, recv, device):
    return pltpu.make_async_remote_copy(
        src_ref=src, dst_ref=dst, send_sem=send, recv_sem=recv, device_id=device, device_id_type=MESH
    )


def enter(targets):
    barrier = pltpu.get_barrier_semaphore()
    for target in targets:
        pl.semaphore_signal(barrier, inc=1, device_id=target, device_id_type=MESH)
    pl.semaphore_wait(barrier, len(targets))


def rsqrt_mean(values):
    return lax.rsqrt(jnp.mean(values * values, axis=-1, keepdims=True) + EPSILON)


def forward_kernel(
    tok_ref, w_ref, rows_ref, kv_out, w_out, proj_ref, tokt_ref,
    tokb, wb, wall, kvb, loc, outs,
    wzs, wzr, wys, wyr, wxs, wxr, wcs, wcr, kzs, kzr, kys, kyr, kcs, kcr,
):
    x, l, y, h, c = place()
    to = peers()
    enter([to[a](d) for a in ("h", "y", "x") for d in (1, 2, 3)] + [to["c"](1)])
    sent = []

    def go(copy):
        copy.start()
        sent.append(copy)

    def w_x(d, yy):
        return remote(
            wb.at[c, x, yy], wb.at[c, x, yy], wxs.at[d - 1, yy], wxr.at[d - 1, yy], to["x"](d)
        )

    def w_c(xx, yy):
        piece = wb.at[c, xx, yy]
        return remote(piece, piece, wcs.at[xx, yy], wcr.at[xx, yy], to["c"](1))

    own = w_ref.at[pl.ds(pl.multiple_of(x * PIECE, 16), PIECE)]
    mine = pltpu.make_async_copy(own, wb.at[c, x, y, h], loc.at[0])
    mine.start()
    zs = [
        remote(own, wb.at[c, x, y, h], wzs.at[d - 1], wzr.at[d - 1], to["h"](d)) for d in (2, 1, 3)
    ]
    for copy in zs:
        go(copy)
    for b in range(NRB):
        tokb[b] = tok_ref[:, b * BLK : (b + 1) * BLK]
        tokt_ref[b] = tok_ref[:, b * BLK : (b + 1) * BLK].T
    mine.wait()
    for copy in zs:
        copy.wait_recv()
    ys = [
        remote(wb.at[c, x, y], wb.at[c, x, y], wys.at[d - 1], wyr.at[d - 1], to["y"](d))
        for d in (2, 1, 3)
    ]
    for copy in ys:
        go(copy)
    for yy in (3, 0, 1, 2):

        @pl.when(y != yy)
        def _():
            back = (y + 3 - yy) % 4
            remote(
                wb.at[c, x, yy], wb.at[c, x, yy], wys.at[back], wyr.at[back], to["y"](1)
            ).wait_recv()

        for d in (2, 1, 3):
            go(w_x(d, yy))
        go(w_c(x, yy))

    def forward_x(yy):
        for d in (1, 3, 2):
            w_x(d, yy).wait_recv()
            go(w_c((x + 4 - d) % 4, yy))

    def assemble(yy):
        for xx in range(4):
            w_c(xx, yy).wait_recv()
        for cc in range(2):
            for hh in range(4):
                for q in range(4):
                    row = ((yy * 4 + hh) * 2 + cc) * SHARD + q * PIECE
                    wall[row : row + PIECE, :] = wb[cc, q, yy, hh]

    def project(col):
        chosen = jnp.concatenate(
            [tokb[rows_ref[col, r]] for r in range(NBR)], axis=1
        )
        rows = NBR * BLK
        return jnp.dot(
            chosen, wall[col * rows : (col + 1) * rows, :], preferred_element_type=F32
        ).astype(BF)

    forward_x(3)
    assemble(3)
    key = project(QPG)
    value = project(QPG + 1)
    proj_ref[QPG] = key
    proj_ref[QPG + 1] = value
    wide = key.astype(F32)
    kvb[c, y, h, 0:128, :] = (wide * rsqrt_mean(wide)).astype(BF)
    kvb[c, y, h, 128:256, :] = value

    def k_y(d, hh):
        piece = kvb.at[c, y, hh]
        return remote(piece, piece, kys.at[d - 1, hh], kyr.at[d - 1, hh], to["y"](d))

    def k_c(yy, hh):
        piece = kvb.at[c, yy, hh]
        return remote(piece, piece, kcs.at[yy, hh], kcr.at[yy, hh], to["c"](1))

    kz = [
        remote(kvb.at[c, y, h], kvb.at[c, y, h], kzs.at[d - 1], kzr.at[d - 1], to["h"](d))
        for d in (1, 2, 3)
    ]
    for d in (2, 1, 3):
        go(kz[d - 1])
    for d in (2, 1, 3):
        go(k_y(d, h))
    go(k_c(y, h))
    for yy in (0, 1, 2):
        forward_x(yy)
    for d in (1, 3, 2):
        kz[d - 1].wait_recv()
        hh = (h + 4 - d) % 4
        for e in (2, 1, 3):
            go(k_y(e, hh))
        go(k_c(y, hh))
    for yy in (0, 1, 2):
        assemble(yy)
    save_w = pltpu.make_async_copy(wall, w_out, loc.at[1])
    save_w.start()
    for col in range(QPG):
        proj_ref[col] = project(col)
    for step in (0, 1, 3, 2):
        hh = (h + 4 - step) % 4
        for d in (1, 3, 2):
            k_y(d, hh).wait_recv()
            go(k_c((y + 4 - d) % 4, hh))
    saves = []
    for step in (0, 1, 3, 2):
        hh = (h + 4 - step) % 4
        for yy in range(4):
            k_c(yy, hh).wait_recv()
    for cc in range(2):
        save = pltpu.make_async_copy(kvb.at[cc], kv_out.at[cc], outs.at[cc])
        save.start()
        saves.append(save)
    for copy in sent:
        copy.wait_send()
    for save in saves:
        save.wait()
    save_w.wait()


def attention_kernel(
    pairs_ref, kv_ref, proj_ref, up_ref, gp_ref, dkv_ref,
    ks, vs, kt, vt, es, dk, dv, qh, qt, gg, gt, dd, acc, tot,
):
    me = lax.axis_index("ctx")

    def gather(owner, _):
        spot = (owner % 2) * 16 + owner // 2
        for part in range(2):
            at = pl.multiple_of(pairs_ref[owner, part] * SPAN, SPAN)
            ks[pl.ds(at, SPAN), :] = kv_ref[spot, part * SPAN : (part + 1) * SPAN, :]
            vs[pl.ds(at, SPAN), :] = kv_ref[spot, 128 + part * SPAN : 128 + (part + 1) * SPAN, :]
        return 0

    lax.fori_loop(0, 32, gather, 0)

    def chunks(part):
        return ((pairs_ref[me, part] + 1) * SPAN + CHUNK - 1) // CHUNK

    def rows_of(index):
        return pl.ds(pl.multiple_of(index * CHUNK, CHUNK), CHUNK)

    def flip(index, _):
        kt[index] = ks[rows_of(index), :].T
        vt[index] = vs[rows_of(index), :].T
        return 0

    lax.fori_loop(0, chunks(1), flip, 0)

    def part_rows(part, head):
        return slice(head * SPAN, (head + 1) * SPAN), slice(part * SPAN, (part + 1) * SPAN)

    for part in range(2):
        for head in range(QPG):
            put, get = part_rows(part, head)
            raw = proj_ref[head, get, :].astype(F32)
            qh[part, put, :] = (raw * rsqrt_mean(raw)).astype(BF)
            gg[part, put, :] = up_ref[get, head * HD : (head + 1) * HD]
        qt[part] = qh[part].T

    factor = SCALE * math.log2(math.e)

    def forward(part):
        count = chunks(part)
        acc[...] = jnp.zeros_like(acc)
        tot[...] = jnp.zeros_like(tot)

        def tile(index, masked):
            score = jnp.dot(ks[rows_of(index), :], qt[part], preferred_element_type=F32)
            expo = jnp.exp2(score * factor)
            if masked:
                key_pos = index * CHUNK + lax.broadcasted_iota(jnp.int32, expo.shape, 0)
                query_pos = pairs_ref[me, part] * SPAN + lax.broadcasted_iota(
                    jnp.int32, expo.shape, 1
                ) % SPAN
                expo = jnp.where(key_pos <= query_pos, expo, 0.0)
            tot[...] += jnp.sum(expo.reshape(CHUNK // 8, 8, expo.shape[1]), axis=0)
            low = expo.astype(BF)
            es[part * 8 + index] = low
            acc[...] += jnp.dot(vt[index], low, preferred_element_type=F32)

        def step(index, _):
            tile(index, False)
            return 0

        lax.fori_loop(0, count - 1, step, 0)
        tile(count - 1, True)
        inverse = 1.0 / jnp.sum(tot[...], axis=0, keepdims=True)
        up = gg[part].astype(F32).T
        delta = jnp.sum(up * (acc[...] * inverse), axis=0, keepdims=True)
        scaled = inverse * SCALE
        low = (up * scaled).astype(BF)
        gt[part] = low
        gg[part] = low.T
        dd[part] = jnp.broadcast_to(delta * scaled, dd.shape[1:])

    def backward(part, first):
        count = chunks(part)
        acc[...] = jnp.zeros_like(acc)

        def step(index, _):
            low = es[part * 8 + index]
            dprob = jnp.dot(vs[rows_of(index), :], gt[part], preferred_element_type=F32)
            dscore = (low.astype(F32) * (dprob - dd[part, 0:1, :])).astype(BF)
            more_k = jnp.dot(dscore, qh[part], preferred_element_type=F32)
            more_v = jnp.dot(low, gg[part], preferred_element_type=F32)
            if first:
                dk[rows_of(index), :] = more_k
                dv[rows_of(index), :] = more_v
            else:
                dk[rows_of(index), :] += more_k
                dv[rows_of(index), :] += more_v
            acc[...] += jnp.dot(kt[index], dscore, preferred_element_type=F32)
            return 0

        lax.fori_loop(0, count, step, 0)
        grad = acc[...].T
        for head in range(QPG):
            put, get = part_rows(part, head)
            up = grad[put, :]
            raw = proj_ref[head, get, :].astype(F32)
            rq = rsqrt_mean(raw)
            gp_ref[head, get, :] = (
                rq * up - raw * (rq * rq * rq) * jnp.mean(up * raw, axis=-1, keepdims=True)
            ).astype(BF)

    forward(1)
    forward(0)
    backward(1, True)
    backward(0, False)

    def clear(index, _):
        dk[rows_of(index), :] = jnp.zeros((CHUNK, HD), F32)
        dv[rows_of(index), :] = jnp.zeros((CHUNK, HD), F32)
        return 0

    lax.fori_loop(chunks(1), 4096 // CHUNK, clear, 0)

    def scatter(owner, _):
        spot = (owner % 2) * 16 + owner // 2
        for part in range(2):
            at = pl.multiple_of(pairs_ref[owner, part] * SPAN, SPAN)
            low = part * SPAN
            dkv_ref[spot, low : low + SPAN, :] = dk[pl.ds(at, SPAN), :].astype(BF)
            dkv_ref[spot, 128 + low : 128 + low + SPAN, :] = (
                dv[pl.ds(at, SPAN), :] * math.sqrt(HD)
            ).astype(BF)
        return 0

    lax.fori_loop(0, 32, scatter, 0)


def reduce_kernel(
    dkv_ref, gpq_ref, proj_ref, tokt_ref, rows_ref, gw_ref, gpkv_ref,
    rc, sb, ry, s2, rz, pw, wc, sx, rx, ty, wy, tz, wz, tl, rl, og,
    dcs, dcr, dys, dyr, dzs, dzr, pcs, pcr, pxs, pxr, pys, pyr, pzs, pzr, pls, plr, pgs, pgr,
):
    x, l, y, h, c = place()
    to = peers()
    enter([to[a](d) for a in ("h", "y", "x", "l") for d in (1, 2, 3)] + [to["c"](1)])
    sent = []

    def go(copy):
        copy.start()
        sent.append(copy)

    def d_c(yy):
        return remote(dkv_ref.at[1 - c, yy], rc.at[yy], dcs.at[yy], dcr.at[yy], to["c"](1))

    for d in (2, 1, 3, 0):
        go(d_c((y + d) % 4))

    def partial(col, grad):
        chosen = jnp.concatenate([tokt_ref[rows_ref[col, r]] for r in range(NBR)], axis=0)
        rows = NBR * BLK
        pw[col * rows : (col + 1) * rows, :] = jnp.dot(
            chosen, grad, preferred_element_type=F32
        ).astype(BF)

    def d_y(d, hh):
        return remote(
            sb.at[(y + d) % 4, hh], ry.at[d - 1, hh], dys.at[d - 1, hh], dyr.at[d - 1, hh], to["y"](d)
        )

    for d in (2, 1, 3, 0):
        yy = (y + d) % 4
        d_c(yy).wait_recv()
        for step in (2, 1, 3, 0):
            hh = (h + step) % 4
            sb[yy, hh] = (dkv_ref[c, yy, hh].astype(F32) + rc[yy, hh].astype(F32)).astype(BF)
            if d:
                go(d_y(d, hh))

    def p_c(yy, hh):
        row = ((yy * 4 + hh) * 2 + 1 - c) * SHARD
        return remote(
            pw.at[pl.ds(pl.multiple_of(row, 64), SHARD)],
            wc.at[yy, hh],
            pcs.at[yy, hh],
            pcr.at[yy, hh],
            to["c"](1),
        )

    for col in range(QPG):
        partial(col, gpq_ref[col])
    for yy in (0, 1, 2):
        for hh in range(4):
            go(p_c(yy, hh))

    d_z = [
        remote(s2.at[(h + d) % 4], rz.at[d - 1], dzs.at[d - 1], dzr.at[d - 1], to["h"](d))
        for d in (1, 2, 3)
    ]
    for step in (2, 1, 3, 0):
        hh = (h + step) % 4
        total = sb[y, hh].astype(F32)
        for d in (1, 3, 2):
            d_y(d, hh).wait_recv()
            total = total + ry[d - 1, hh].astype(F32)
        s2[hh] = total.astype(BF)
        if step:
            go(d_z[step - 1])

    def p_x(d, yy):
        return remote(
            sx.at[(x + d) % 4, yy], rx.at[d - 1, yy], pxs.at[d - 1, yy], pxr.at[d - 1, yy], to["x"](d)
        )

    def fold_core(yy):
        for hh in range(4):
            p_c(yy, hh).wait_recv()
            row = pl.multiple_of(((yy * 4 + hh) * 2 + c) * SHARD, 64)
            for q in range(4):
                sx[q, yy, hh] = (
                    pw[pl.ds(row + q * PIECE, PIECE), :].astype(F32)
                    + wc[yy, hh, q * PIECE : (q + 1) * PIECE, :].astype(F32)
                ).astype(BF)
        for d in (2, 1, 3):
            go(p_x(d, yy))

    def p_y(yy):
        d = (yy + 3 - y) % 4
        return remote(ty.at[yy], wy.at[d], pys.at[yy], pyr.at[d], (l * 4 + x, yy * 8 + h * 2 + c))

    def fold_x(yy):
        total = sx[x, yy].astype(F32)
        for d in (1, 3, 2):
            p_x(d, yy).wait_recv()
            total = total + rx[d - 1, yy].astype(F32)
        ty[yy] = total.astype(BF)

        @pl.when(y != yy)
        def _():
            p_y(yy).start()

    p_z = [
        remote(tz.at[(h + d) % 4], wz.at[d - 1], pzs.at[d - 1], pzr.at[d - 1], to["h"](d))
        for d in (1, 2, 3)
    ]
    p_l = [
        remote(tl, rl.at[d - 1], pls.at[d - 1], plr.at[d - 1], to["l"](d)) for d in (1, 2, 3)
    ]
    p_g = [
        remote(og.at[x], og.at[x], pgs.at[d - 1], pgr.at[d - 1], to["x"](d)) for d in (1, 2, 3)
    ]

    def finish():
        total = ty[y].astype(F32)
        for d in (1, 3, 2):
            remote(ty.at[0], wy.at[d - 1], pys.at[0], pyr.at[d - 1], to["y"](1)).wait_recv()
            total = total + wy[d - 1].astype(F32)
        tz[...] = total.astype(BF)
        for d in (2, 1, 3):
            p_z[d - 1].start()
        total = tz[h].astype(F32)
        for d in (1, 3, 2):
            p_z[d - 1].wait_recv()
            total = total + wz[d - 1].astype(F32)
        tl[...] = total
        for d in (2, 1, 3):
            p_l[d - 1].start()
        for d in (1, 3, 2):
            p_l[d - 1].wait_recv()
            total = total + rl[d - 1]
        og[x] = total
        for d in (2, 1, 3):
            p_g[d - 1].start()

    for yy in (0, 1, 2):
        fold_core(yy)
    total = s2[h].astype(F32)
    for d in (1, 3, 2):
        d_z[d - 1].wait_recv()
        total = total + rz[d - 1].astype(F32)
    up = total[0:128]
    raw = proj_ref[QPG].astype(F32)
    rk = rsqrt_mean(raw)
    grad_key = (
        rk * up - raw * (rk * rk * rk) * jnp.mean(up * raw, axis=-1, keepdims=True)
    ).astype(BF)
    grad_value = total[128:256].astype(BF)
    gpkv_ref[0] = grad_key
    gpkv_ref[1] = grad_value
    partial(QPG, grad_key)
    partial(QPG + 1, grad_value)
    for hh in range(4):
        go(p_c(3, hh))
    for yy in (0, 1, 2):
        fold_x(yy)
    fold_core(3)
    fold_x(3)
    finish()
    for copy in p_g:
        copy.wait_recv()
    for q in range(4):
        gw_ref[q * PIECE : (q + 1) * PIECE, :] = og[q]
    for copy in sent + p_z + p_l + p_g:
        copy.wait_send()
    for yy in range(4):

        @pl.when(y != yy)
        def _():
            p_y(yy).wait_send()


def tokens_kernel(gpq_ref, gpkv_ref, w_ref, rows_ref, out_ref, acc):
    rows = NBR * BLK
    for col in range(NCB):
        grad = gpq_ref[col] if col < QPG else gpkv_ref[col - QPG]
        spread = lax.dot_general(
            grad,
            w_ref[col * rows : (col + 1) * rows, :],
            (((1,), (1,)), ((), ())),
            preferred_element_type=F32,
        )
        for r in range(NBR):
            at = pl.ds(pl.multiple_of(rows_ref[col, r] * BLK, BLK), BLK)
            piece = spread[:, r * BLK : (r + 1) * BLK]
            if col < NRB // NBR:
                acc[:, at] = piece
            else:
                acc[:, at] += piece
    out_ref[...] = acc[...].astype(BF)


VM = pl.BlockSpec(memory_space=pltpu.VMEM)
SM = pl.BlockSpec(memory_space=pltpu.SMEM)
HB = pl.BlockSpec(memory_space=pl.ANY)
LIMIT = 60 * 1024 * 1024


def dma(*shape):
    return pltpu.SemaphoreType.DMA(shape)


def shape(dims, kind=BF):
    return jax.ShapeDtypeStruct(dims, kind)


def run_forward(tokens, w, block_rows):
    return pl.pallas_call(
        forward_kernel,
        out_shape=(
            shape((2, 4, 4, 256, HD)),
            shape((NCB * NBR * BLK, BLK)),
            shape((NCB, 128, HD)),
            shape((NRB, BLK, 128)),
        ),
        in_specs=[VM, VM, SM],
        out_specs=(HB, HB, VM, VM),
        scratch_shapes=[
            pltpu.VMEM((NRB, 128, BLK), BF),
            pltpu.VMEM((2, 4, 4, 4, PIECE, BLK), BF),
            pltpu.VMEM((NCB * NBR * BLK, BLK), BF),
            pltpu.VMEM((2, 4, 4, 256, HD), BF),
            dma(2), dma(2),
            dma(3), dma(3), dma(3), dma(3), dma(3, 4), dma(3, 4), dma(4, 4), dma(4, 4),
            dma(3), dma(3), dma(3, 4), dma(3, 4), dma(4, 4), dma(4, 4),
        ],
        compiler_params=pltpu.CompilerParams(
            collective_id=0, has_side_effects=True, vmem_limit_bytes=LIMIT
        ),
        name="forward",
    )(tokens, w, block_rows)


def run_attention(pairs, kv, proj, upstream):
    rows = QPG * SPAN
    return pl.pallas_call(
        attention_kernel,
        out_shape=(shape((QPG, 128, HD)), shape((32, 256, HD))),
        in_specs=[SM, VM, VM, VM],
        out_specs=(VM, VM),
        scratch_shapes=[
            pltpu.VMEM((4096, HD), BF),
            pltpu.VMEM((4096, HD), BF),
            pltpu.VMEM((16, HD, CHUNK), BF),
            pltpu.VMEM((16, HD, CHUNK), BF),
            pltpu.VMEM((24, CHUNK, rows), BF),
            pltpu.VMEM((4096, HD), F32),
            pltpu.VMEM((4096, HD), F32),
            pltpu.VMEM((2, rows, HD), BF),
            pltpu.VMEM((2, HD, rows), BF),
            pltpu.VMEM((2, rows, HD), BF),
            pltpu.VMEM((2, HD, rows), BF),
            pltpu.VMEM((2, 8, rows), F32),
            pltpu.VMEM((HD, rows), F32),
            pltpu.VMEM((8, rows), F32),
        ],
        compiler_params=pltpu.CompilerParams(vmem_limit_bytes=LIMIT),
        name="attention",
    )(pairs, kv, proj, upstream)


def run_reduce(dkv, gpq, proj, tokt, block_rows):
    return pl.pallas_call(
        reduce_kernel,
        out_shape=(shape((SHARD, BLK), F32), shape((2, 128, HD))),
        in_specs=[VM, VM, VM, VM, SM],
        out_specs=(VM, VM),
        scratch_shapes=[
            pltpu.VMEM((4, 4, 256, HD), BF),
            pltpu.VMEM((4, 4, 256, HD), BF),
            pltpu.VMEM((3, 4, 256, HD), BF),
            pltpu.VMEM((4, 256, HD), BF),
            pltpu.VMEM((3, 256, HD), BF),
            pltpu.VMEM((NCB * NBR * BLK, BLK), BF),
            pltpu.VMEM((4, 4, SHARD, BLK), BF),
            pltpu.VMEM((4, 4, 4, PIECE, BLK), BF),
            pltpu.VMEM((3, 4, 4, PIECE, BLK), BF),
            pltpu.VMEM((4, 4, PIECE, BLK), BF),
            pltpu.VMEM((3, 4, PIECE, BLK), BF),
            pltpu.VMEM((4, PIECE, BLK), BF),
            pltpu.VMEM((3, PIECE, BLK), BF),
            pltpu.VMEM((PIECE, BLK), F32),
            pltpu.VMEM((3, PIECE, BLK), F32),
            pltpu.VMEM((4, PIECE, BLK), F32),
            dma(4), dma(4), dma(3, 4), dma(3, 4), dma(3), dma(3),
            dma(4, 4), dma(4, 4), dma(3, 4), dma(3, 4), dma(4), dma(3),
            dma(3), dma(3), dma(3), dma(3), dma(3), dma(3),
        ],
        compiler_params=pltpu.CompilerParams(
            collective_id=1, has_side_effects=True, vmem_limit_bytes=LIMIT
        ),
        name="reduce",
    )(dkv, gpq, proj, tokt, block_rows)


def run_tokens(gpq, gpkv, w_all, block_rows):
    return pl.pallas_call(
        tokens_kernel,
        out_shape=shape((128, D)),
        in_specs=[VM, VM, VM, SM],
        out_specs=VM,
        scratch_shapes=[pltpu.VMEM((128, D), F32)],
        compiler_params=pltpu.CompilerParams(vmem_limit_bytes=LIMIT),
        name="tokens",
    )(gpq, gpkv, w_all, block_rows)


def per_device(tokens, grad_attn, w_packed, block_rows, span_pairs):
    kv, w_all, proj, tokt = run_forward(tokens[0], w_packed, block_rows)
    gpq, dkv = run_attention(span_pairs, kv.reshape(32, 256, HD), proj, grad_attn[0])
    grad_weights, gpkv = run_reduce(dkv.reshape(2, 4, 4, 256, HD), gpq, proj, tokt, block_rows)
    grad_tokens = run_tokens(gpq, gpkv, w_all, block_rows)
    return (grad_tokens[None], grad_weights)


def solution(mesh):
    in_specs = (P("dp", "ctx", None), P("dp", "ctx", None), P("ctx", None), P(), P())
    out_specs = (P("dp", "ctx", None), P("ctx", None))
    return jax.shard_map(
        per_device, mesh=mesh, in_specs=in_specs, out_specs=out_specs, check_vma=False
    )
```

time: 902 us -> 160 us (0.18)
  waiting for transfers between devices: 673 us -> 0 us
  Pallas kernels: 0 us -> 155 us
  local copies, waits for them, and re-layouts: 95.3 us -> 3.39 us
  matrix products: 87.8 us -> 0 us
  other arithmetic: 16.5 us -> 0 us
  between operations: 15.8 us -> 0.66 us
  starting transfers between devices: 10.2 us -> 0 us
    reduce_scatter x2 -> x0, waiting for transfers between devices: 235 us -> none  [the longest x1 120 us: per_device(): lax.psum_scatter(owner_values, 'ctx', scatter_dimension=0, tiled=True)]
    all_gather x3 -> x0, waiting for transfers between devices: 180 us -> none  [the longest x1 80.8 us: per_device(): lax.all_gather(w_packed, 'ctx', axis=0, tiled=True)]
    pallas_call x0 -> x4, Pallas kernels: none -> 155 us  [the longest x1 70.2 us: run_reduce(): pl.pallas_call(reduce_kernel, out_shape=(shape((SHARD, BLK), F32), shape(...]
    psum x1 -> x0, waiting for transfers between devices: 145 us -> none  [per_device(): grad_weights = lax.psum(summed, 'dp')]
    all_to_all x1 -> x0, waiting for transfers between devices: 112 us -> none  [per_device(): lax.all_to_all(partial_w, 'ctx', split_axis=0, concat_axis=0, tiled=True)]
    dot_general x67 -> x0, matrix products: 87.8 us -> none  [the longest x9 17.9 us: backward_tile(): jnp.einsum('tgqu,tgqd->ugd', dscore, query_part, preferred_element_type=j...]
    gather x6 -> x0, local copies, waits for them, and re-layouts: 67.1 us -> none  [the longest x1 15.8 us: per_device(): owner_keys = jnp.take(grad_keys_all, all_positions, axis=0)]
    scatter x1 -> x0, local copies, waits for them, and re-layouts: 15.5 us -> none  [per_device(): jnp.zeros((length,), jnp.int32).at[all_positions]]
  transfers between devices with their start and end apart: 7 -> 0, of which waited for: 7 -> 0; matrix products, arithmetic and copies ran while one was open for 7% -> 0% of each run, Pallas kernels for 0% -> 0%
where the time goes in v1:
time: 160 us; the launch traced here: 159 us
  Pallas kernels  155 us (97%)
  local copies, waits for them, and re-layouts  3.39 us (2%)
    pallas_call x1, Pallas kernels, run_reduce(): pl.pallas_call(reduce_kernel, out_shape=(shape((SHARD, BLK), F32), shape(...  70.2 us
    pallas_call x1, Pallas kernels, run_forward(): pl.pallas_call(forward_kernel, out_shape=(shape((2, 4, 4, 256, HD)), shap...  60.1 us
    pallas_call x1, Pallas kernels, run_attention(): pl.pallas_call(attention_kernel, out_shape=(shape((QPG, 128, HD)), shape(...  20.9 us
    pallas_call x1, Pallas kernels, run_tokens(): pl.pallas_call(tokens_kernel, out_shape=shape((128, D)), in_specs=[VM, VM...  4.25 us
    unnamed x5, local copies, waits for them, and re-layouts  3.39 us

profile of v1, /device:TPU:24, one launch (start us, length us, event | category | flops | bytes accessed | tf_op | source)
XLA Modules:
  0.0 159.5 jit_solution(2058114943897852559)
XLA Ops:
  0.6 1.4 copy.7.rows_ref
  2.0 1.4 copy.8.pairs_ref
  3.4 60.1 %forward.1 = (bf16[2,4,4,256,128]{4,3,2,1,0:T(8,128)(2,1)}, bf16[10240,128]{1,0:T(8,128)(2,1)}, bf16[10,128,128]{2,1,0:T(8,128)(2,1)}, bf16[32,128,128]{2,1,0:T(8,128)(2,1)}) custom-call(bf16[128,4096]{1,0:T(8,128)(2,1)} %bitcast.7, bf16[320,128]{1,0:T(8,128)(2,1)} %w_ref.1, s32[10,8]{1,0:T(8,128)} %copy.7.rows_ref), custom_call_target="tpu_custom_call" | custom-call | tf_op jit(solution)/shard_map/forward/pallas_call | solution.py:548
  63.5 20.9 %attention.1 = (bf16[8,128,128]{2,1,0:T(8,128)(2,1)}, bf16[32,256,128]{2,1,0:T(8,128)(2,1)}) custom-call(s32[32,2]{1,0:T(8,128)} %copy.8.pairs_ref, bf16[32,256,128]{2,1,0:T(8,128)(2,1)} %bitcast.6, bf16[10,128,128]{2,1,0:T(8,128)(2,1)} %get-tuple-element.11.proj_ref, bf16[128,1024]{1,0:T(8,128)(2,1)} %bitcast.9), custom_call_target="tpu_custom_call" | custom-call | tf_op jit(solution)/shard_map/attention/pallas_call | solution.py:576
  84.4 70.2 %reduce.1 = (f32[320,128]{1,0:T(8,128)}, bf16[2,128,128]{2,1,0:T(8,128)(2,1)}) custom-call(bf16[2,4,4,256,128]{4,3,2,1,0:T(8,128)(2,1)} %bitcast.5, bf16[8,128,128]{2,1,0:T(8,128)(2,1)} %get-tuple-element.12.gpq_ref, bf16[10,128,128]{2,1,0:T(8,128)(2,1)} %get-tuple-element.11.proj_ref, bf16[32,128,128]{2,1,0:T(8,128)(2,1)} %get-tuple-element.14.tokt_ref, ...), custom_call_target="tpu_custom_call" | custom-call | tf_op jit(solution)/shard_map/reduce/pallas_call | solution.py:603
  154.5 0.0 copy-start
  154.6 4.3 %tokens.1 = bf16[128,4096]{1,0:T(8,128)(2,1)} custom-call(bf16[8,128,128]{2,1,0:T(8,128)(2,1)} %get-tuple-element.12.gpq_ref, bf16[2,128,128]{2,1,0:T(8,128)(2,1)} %get-tuple-element.15.gpkv_ref, bf16[10240,128]{1,0:T(8,128)(2,1)} %get-tuple-element.16.w_ref, s32[10,8]{1,0:T(8,128)} %copy.7.rows_ref), custom_call_target="tpu_custom_call" | custom-call | tf_op jit(solution)/shard_map/tokens/pallas_call | solution.py:637
  158.8 0.0 copy-done
  158.8 0.7 copy.12
Async XLA Ops:
  154.5 4.3 %copy-start = (f32[320,128]{1,0:T(8,128)S(1)}, f32[320,128]{1,0:T(8,128)}, u32[]{:S(2)}) copy-start(f32[320,128]{1,0:T(8,128)} %get-tuple-element.21) | copy-start | bytes 491524

commit v2 on v1

--- a/solution.py
+++ b/solution.py
@@ -20,7 +20,7 @@
 SCALE = 1.0 / math.sqrt(HD)
 SHARD = 320
 PIECE = 80
-CHUNK = 256
+CHUNK = 512
 BF = jnp.bfloat16
 F32 = jnp.float32
 MESH = pl.DeviceIdType.MESH
@@ -60,18 +60,80 @@
     pl.semaphore_wait(barrier, len(targets))
 
 
+class Ring:
+    def __init__(self, own, at, send, recv):
+        to = peers()
+        h = place()[3]
+        up, down = to["h"](1), to["h"](3)
+        self.own = [
+            remote(own(0), at(h, 0), send.at[0], recv.at[0], up),
+            remote(own(1), at(h, 1), send.at[1], recv.at[1], down),
+            remote(own(1), at(h, 1), send.at[2], recv.at[2], up),
+            remote(own(0), at(h, 0), send.at[3], recv.at[3], down),
+        ]
+        before, after = at((h + 3) % 4, 0), at((h + 1) % 4, 1)
+        self.relay = [
+            remote(before, before, send.at[4], recv.at[4], up),
+            remote(after, after, send.at[5], recv.at[5], down),
+        ]
+
+
+class RingSum:
+    def __init__(self, terms, relayed, landed, halves, send, recv):
+        to = peers()
+        self.h = place()[3]
+        up, down = to["h"](1), to["h"](3)
+        self.terms, self.relayed, self.landed, self.halves = terms, relayed, landed, halves
+        h, (a, b) = self.h, halves
+        far, nxt, prev = (h + 2) % 4, (h + 1) % 4, (h + 3) % 4
+        self.first = [
+            remote(terms.at[far, a], relayed.at[a], send.at[0], recv.at[0], up),
+            remote(terms.at[far, b], relayed.at[b], send.at[1], recv.at[1], down),
+        ]
+        self.direct = [
+            remote(terms.at[nxt, b], landed.at[0, b], send.at[2], recv.at[2], up),
+            remote(terms.at[prev, a], landed.at[1, a], send.at[3], recv.at[3], down),
+        ]
+        self.added = [
+            remote(terms.at[nxt, a], landed.at[0, a], send.at[4], recv.at[4], up),
+            remote(terms.at[prev, b], landed.at[1, b], send.at[5], recv.at[5], down),
+        ]
+
+    def pass_on(self, go):
+        h, (a, b) = self.h, self.halves
+        for index, half, target in ((0, a, (h + 1) % 4), (1, b, (h + 3) % 4)):
+            self.first[index].wait_recv()
+            self.terms[target, half] = (
+                self.terms[target, half].astype(F32) + self.relayed[half].astype(F32)
+            ).astype(BF)
+            go(self.added[index])
+
+    def result(self):
+        for copy in self.direct + self.added:
+            copy.wait_recv()
+        return (
+            self.terms[self.h].astype(F32)
+            + self.landed[0].astype(F32)
+            + self.landed[1].astype(F32)
+        )
+
+
 def rsqrt_mean(values):
     return lax.rsqrt(jnp.mean(values * values, axis=-1, keepdims=True) + EPSILON)
 
 
 def forward_kernel(
-    tok_ref, w_ref, rows_ref, kv_out, w_out, proj_ref, tokt_ref,
-    tokb, wb, wall, kvb, loc, outs,
+    tok_ref, w_ref, table_ref, kv_out, w_out, proj_ref, tokt_ref,
+    rows_ref, tokb, wb, wall, kvb, loc, outs,
     wzs, wzr, wys, wyr, wxs, wxr, wcs, wcr, kzs, kzr, kys, kyr, kcs, kcr,
 ):
     x, l, y, h, c = place()
     to = peers()
-    enter([to[a](d) for a in ("h", "y", "x") for d in (1, 2, 3)] + [to["c"](1)])
+    table = pltpu.make_async_copy(table_ref, rows_ref, loc.at[2])
+    table.start()
+    enter(
+        [to[a](d) for a in ("y", "x") for d in (1, 2, 3)] + [to["h"](1), to["h"](3), to["c"](1)]
+    )
     sent = []
 
     def go(copy):
@@ -87,26 +149,38 @@
         piece = wb.at[c, xx, yy]
         return remote(piece, piece, wcs.at[xx, yy], wcr.at[xx, yy], to["c"](1))
 
-    own = w_ref.at[pl.ds(pl.multiple_of(x * PIECE, 16), PIECE)]
-    mine = pltpu.make_async_copy(own, wb.at[c, x, y, h], loc.at[0])
+    row = pl.multiple_of(x * PIECE, 16)
+    mine = pltpu.make_async_copy(w_ref.at[pl.ds(row, PIECE)], wb.at[c, x, y, h], loc.at[0])
     mine.start()
-    zs = [
-        remote(own, wb.at[c, x, y, h], wzs.at[d - 1], wzr.at[d - 1], to["h"](d)) for d in (2, 1, 3)
-    ]
-    for copy in zs:
+    w_cut = ((0, 48), (48, 32))
+    wz = Ring(
+        lambda half: w_ref.at[pl.ds(row + w_cut[half][0], w_cut[half][1])],
+        lambda hh, half: wb.at[c, x, y, hh, pl.ds(*w_cut[half])],
+        wzs,
+        wzr,
+    )
+    for copy in wz.own:
         go(copy)
     for b in range(NRB):
         tokb[b] = tok_ref[:, b * BLK : (b + 1) * BLK]
         tokt_ref[b] = tok_ref[:, b * BLK : (b + 1) * BLK].T
     mine.wait()
-    for copy in zs:
+    for index in range(2):
+        wz.own[index].wait_recv()
+        go(wz.relay[index])
+    for copy in wz.own[2:] + wz.relay:
         copy.wait_recv()
     ys = [
         remote(wb.at[c, x, y], wb.at[c, x, y], wys.at[d - 1], wyr.at[d - 1], to["y"](d))
         for d in (2, 1, 3)
     ]
-    for copy in ys:
-        go(copy)
+    sent.extend(ys)
+
+    @pl.when(y == 3)
+    def _():
+        for copy in ys:
+            copy.start()
+
     for yy in (3, 0, 1, 2):
 
         @pl.when(y != yy)
@@ -119,6 +193,12 @@
         for d in (2, 1, 3):
             go(w_x(d, yy))
         go(w_c(x, yy))
+        if yy == 3:
+
+            @pl.when(y != 3)
+            def _():
+                for copy in ys:
+                    copy.start()
 
     def forward_x(yy):
         for d in (1, 3, 2):
@@ -136,7 +216,7 @@
 
     def project(col):
         chosen = jnp.concatenate(
-            [tokb[rows_ref[col, r]] for r in range(NBR)], axis=1
+            [tokb[rows_ref[r, col]] for r in range(NBR)], axis=1
         )
         rows = NBR * BLK
         return jnp.dot(
@@ -144,6 +224,7 @@
         ).astype(BF)
 
     forward_x(3)
+    table.wait()
     assemble(3)
     key = project(QPG)
     value = project(QPG + 1)
@@ -161,19 +242,26 @@
         piece = kvb.at[c, yy, hh]
         return remote(piece, piece, kcs.at[yy, hh], kcr.at[yy, hh], to["c"](1))
 
-    kz = [
-        remote(kvb.at[c, y, h], kvb.at[c, y, h], kzs.at[d - 1], kzr.at[d - 1], to["h"](d))
-        for d in (1, 2, 3)
-    ]
-    for d in (2, 1, 3):
-        go(kz[d - 1])
+    k_cut = ((0, 128), (128, 128))
+    kz = Ring(
+        lambda half: kvb.at[c, y, h, pl.ds(*k_cut[half])],
+        lambda hh, half: kvb.at[c, y, hh, pl.ds(*k_cut[half])],
+        kzs,
+        kzr,
+    )
+    for copy in kz.own:
+        go(copy)
     for d in (2, 1, 3):
         go(k_y(d, h))
     go(k_c(y, h))
     for yy in (0, 1, 2):
         forward_x(yy)
+    for index in range(2):
+        kz.own[index].wait_recv()
+        go(kz.relay[index])
     for d in (1, 3, 2):
-        kz[d - 1].wait_recv()
+        for copy in {1: (kz.own[2],), 3: (kz.own[3],), 2: kz.relay}[d]:
+            copy.wait_recv()
         hh = (h + 4 - d) % 4
         for e in (2, 1, 3):
             go(k_y(e, hh))
@@ -194,10 +282,10 @@
         hh = (h + 4 - step) % 4
         for yy in range(4):
             k_c(yy, hh).wait_recv()
-    for cc in range(2):
-        save = pltpu.make_async_copy(kvb.at[cc], kv_out.at[cc], outs.at[cc])
-        save.start()
-        saves.append(save)
+        for cc in range(2):
+            save = pltpu.make_async_copy(kvb.at[cc, :, hh], kv_out.at[cc, :, hh], outs.at[cc, step])
+            save.start()
+            saves.append(save)
     for copy in sent:
         copy.wait_send()
     for save in saves:
@@ -206,23 +294,28 @@
 
 
 def attention_kernel(
-    pairs_ref, kv_ref, proj_ref, up_ref, gp_ref, dkv_ref,
-    ks, vs, kt, vt, es, dk, dv, qh, qt, gg, gt, dd, acc, tot,
+    table_ref, kv_ref, proj_ref, up_ref, gp_ref, dkv_ref,
+    pairs_ref, sems, ks, vs, kt, vt, es, dk, dv, qh, qt, gg, gt, dd, acc, tot,
 ):
     me = lax.axis_index("ctx")
+
+    table = pltpu.make_async_copy(table_ref, pairs_ref, sems.at[0])
+    table.start()
 
     def gather(owner, _):
         spot = (owner % 2) * 16 + owner // 2
         for part in range(2):
-            at = pl.multiple_of(pairs_ref[owner, part] * SPAN, SPAN)
-            ks[pl.ds(at, SPAN), :] = kv_ref[spot, part * SPAN : (part + 1) * SPAN, :]
-            vs[pl.ds(at, SPAN), :] = kv_ref[spot, 128 + part * SPAN : 128 + (part + 1) * SPAN, :]
+            at = pl.ds(pl.multiple_of(pairs_ref[part, owner] * SPAN, SPAN), SPAN)
+            for half, into in ((0, ks), (1, vs)):
+                pltpu.make_async_copy(
+                    kv_ref.at[spot, pl.ds(half * 128 + part * SPAN, SPAN)],
+                    into.at[at],
+                    sems.at[1 + half],
+                ).start()
         return 0
 
-    lax.fori_loop(0, 32, gather, 0)
-
     def chunks(part):
-        return ((pairs_ref[me, part] + 1) * SPAN + CHUNK - 1) // CHUNK
+        return ((pairs_ref[part, me] + 1) * SPAN + CHUNK - 1) // CHUNK
 
     def rows_of(index):
         return pl.ds(pl.multiple_of(index * CHUNK, CHUNK), CHUNK)
@@ -232,11 +325,11 @@
         vt[index] = vs[rows_of(index), :].T
         return 0
 
-    lax.fori_loop(0, chunks(1), flip, 0)
-
     def part_rows(part, head):
         return slice(head * SPAN, (head + 1) * SPAN), slice(part * SPAN, (part + 1) * SPAN)
 
+    table.wait()
+    lax.fori_loop(0, 32, gather, 0)
     for part in range(2):
         for head in range(QPG):
             put, get = part_rows(part, head)
@@ -245,6 +338,9 @@
             gg[part, put, :] = up_ref[get, head * HD : (head + 1) * HD]
         qt[part] = qh[part].T
 
+    pltpu.make_async_copy(ks, ks, sems.at[1]).wait()
+    pltpu.make_async_copy(vs, vs, sems.at[2]).wait()
+    lax.fori_loop(0, chunks(1), flip, 0)
     factor = SCALE * math.log2(math.e)
 
     def forward(part):
@@ -257,13 +353,13 @@
             expo = jnp.exp2(score * factor)
             if masked:
                 key_pos = index * CHUNK + lax.broadcasted_iota(jnp.int32, expo.shape, 0)
-                query_pos = pairs_ref[me, part] * SPAN + lax.broadcasted_iota(
+                query_pos = pairs_ref[part, me] * SPAN + lax.broadcasted_iota(
                     jnp.int32, expo.shape, 1
                 ) % SPAN
                 expo = jnp.where(key_pos <= query_pos, expo, 0.0)
             tot[...] += jnp.sum(expo.reshape(CHUNK // 8, 8, expo.shape[1]), axis=0)
             low = expo.astype(BF)
-            es[part * 8 + index] = low
+            es[part * (2048 // CHUNK) + index] = low
             acc[...] += jnp.dot(vt[index], low, preferred_element_type=F32)
 
         def step(index, _):
@@ -286,7 +382,7 @@
         acc[...] = jnp.zeros_like(acc)
 
         def step(index, _):
-            low = es[part * 8 + index]
+            low = es[part * (2048 // CHUNK) + index]
             dprob = jnp.dot(vs[rows_of(index), :], gt[part], preferred_element_type=F32)
             dscore = (low.astype(F32) * (dprob - dd[part, 0:1, :])).astype(BF)
             more_k = jnp.dot(dscore, qh[part], preferred_element_type=F32)
@@ -326,7 +422,7 @@
     def scatter(owner, _):
         spot = (owner % 2) * 16 + owner // 2
         for part in range(2):
-            at = pl.multiple_of(pairs_ref[owner, part] * SPAN, SPAN)
+            at = pl.multiple_of(pairs_ref[part, owner] * SPAN, SPAN)
             low = part * SPAN
             dkv_ref[spot, low : low + SPAN, :] = dk[pl.ds(at, SPAN), :].astype(BF)
             dkv_ref[spot, 128 + low : 128 + low + SPAN, :] = (
@@ -338,13 +434,21 @@
 
 
 def reduce_kernel(
-    dkv_ref, gpq_ref, proj_ref, tokt_ref, rows_ref, gw_ref, gpkv_ref,
-    rc, sb, ry, s2, rz, pw, wc, sx, rx, ty, wy, tz, wz, tl, rl, og,
+    dkv_ref, gpq_ref, proj_ref, tokens_ref, table_ref, gw_ref, gpkv_ref,
+    rows_ref, tokt_ref, dl, loc, rc, sb, ry, s2, rf, rz, pw, wc, sx, rx, ty, wy, tz, wf, wz, lb, og,
     dcs, dcr, dys, dyr, dzs, dzr, pcs, pcr, pxs, pxr, pys, pyr, pzs, pzr, pls, plr, pgs, pgr,
 ):
     x, l, y, h, c = place()
     to = peers()
-    enter([to[a](d) for a in ("h", "y", "x", "l") for d in (1, 2, 3)] + [to["c"](1)])
+    table = pltpu.make_async_copy(table_ref, rows_ref, loc.at[4])
+    turned = pltpu.make_async_copy(tokens_ref, tokt_ref, loc.at[5])
+    loads = [pltpu.make_async_copy(dkv_ref.at[c, yy], dl.at[yy], loc.at[yy]) for yy in range(4)]
+    for copy in loads + [table, turned]:
+        copy.start()
+    enter(
+        [to[a](d) for a in ("y", "x", "l") for d in (1, 2, 3)]
+        + [to["h"](1), to["h"](3), to["c"](1)]
+    )
     sent = []
 
     def go(copy):
@@ -358,7 +462,7 @@
         go(d_c((y + d) % 4))
 
     def partial(col, grad):
-        chosen = jnp.concatenate([tokt_ref[rows_ref[col, r]] for r in range(NBR)], axis=0)
+        chosen = jnp.concatenate([tokt_ref[rows_ref[r, col]] for r in range(NBR)], axis=0)
         rows = NBR * BLK
         pw[col * rows : (col + 1) * rows, :] = jnp.dot(
             chosen, grad, preferred_element_type=F32
@@ -369,12 +473,14 @@
             sb.at[(y + d) % 4, hh], ry.at[d - 1, hh], dys.at[d - 1, hh], dyr.at[d - 1, hh], to["y"](d)
         )
 
+    for copy in loads:
+        copy.wait()
     for d in (2, 1, 3, 0):
         yy = (y + d) % 4
         d_c(yy).wait_recv()
         for step in (2, 1, 3, 0):
             hh = (h + step) % 4
-            sb[yy, hh] = (dkv_ref[c, yy, hh].astype(F32) + rc[yy, hh].astype(F32)).astype(BF)
+            sb[yy, hh] = (dl[yy, hh].astype(F32) + rc[yy, hh].astype(F32)).astype(BF)
             if d:
                 go(d_y(d, hh))
 
@@ -388,16 +494,15 @@
             to["c"](1),
         )
 
+    table.wait()
+    turned.wait()
     for col in range(QPG):
         partial(col, gpq_ref[col])
     for yy in (0, 1, 2):
         for hh in range(4):
             go(p_c(yy, hh))
 
-    d_z = [
-        remote(s2.at[(h + d) % 4], rz.at[d - 1], dzs.at[d - 1], dzr.at[d - 1], to["h"](d))
-        for d in (1, 2, 3)
-    ]
+    d_z = RingSum(s2, rf, rz, (slice(0, 128), slice(128, 256)), dzs, dzr)
     for step in (2, 1, 3, 0):
         hh = (h + step) % 4
         total = sb[y, hh].astype(F32)
@@ -405,8 +510,12 @@
             d_y(d, hh).wait_recv()
             total = total + ry[d - 1, hh].astype(F32)
         s2[hh] = total.astype(BF)
-        if step:
-            go(d_z[step - 1])
+        if step == 2:
+            for copy in d_z.first:
+                go(copy)
+        elif step:
+            go(d_z.direct[step // 2])
+    d_z.pass_on(go)
 
     def p_x(d, yy):
         return remote(
@@ -440,12 +549,9 @@
         def _():
             p_y(yy).start()
 
-    p_z = [
-        remote(tz.at[(h + d) % 4], wz.at[d - 1], pzs.at[d - 1], pzr.at[d - 1], to["h"](d))
-        for d in (1, 2, 3)
-    ]
+    p_z = RingSum(tz, wf, wz, (slice(0, 48), slice(48, 80)), pzs, pzr)
     p_l = [
-        remote(tl, rl.at[d - 1], pls.at[d - 1], plr.at[d - 1], to["l"](d)) for d in (1, 2, 3)
+        remote(lb.at[l], lb.at[l], pls.at[d - 1], plr.at[d - 1], to["l"](d)) for d in (1, 2, 3)
     ]
     p_g = [
         remote(og.at[x], og.at[x], pgs.at[d - 1], pgr.at[d - 1], to["x"](d)) for d in (1, 2, 3)
@@ -457,28 +563,23 @@
             remote(ty.at[0], wy.at[d - 1], pys.at[0], pyr.at[d - 1], to["y"](1)).wait_recv()
             total = total + wy[d - 1].astype(F32)
         tz[...] = total.astype(BF)
+        for copy in p_z.first + p_z.direct:
+            go(copy)
+        p_z.pass_on(go)
+        lb[l] = p_z.result().astype(BF)
         for d in (2, 1, 3):
-            p_z[d - 1].start()
-        total = tz[h].astype(F32)
-        for d in (1, 3, 2):
-            p_z[d - 1].wait_recv()
-            total = total + wz[d - 1].astype(F32)
-        tl[...] = total
+            go(p_l[d - 1])
+        for copy in p_l:
+            copy.wait_recv()
+        og[x] = (
+            (lb[0].astype(F32) + lb[1].astype(F32)) + (lb[2].astype(F32) + lb[3].astype(F32))
+        ).astype(BF)
         for d in (2, 1, 3):
-            p_l[d - 1].start()
-        for d in (1, 3, 2):
-            p_l[d - 1].wait_recv()
-            total = total + rl[d - 1]
-        og[x] = total
-        for d in (2, 1, 3):
-            p_g[d - 1].start()
+            go(p_g[d - 1])
 
     for yy in (0, 1, 2):
         fold_core(yy)
-    total = s2[h].astype(F32)
-    for d in (1, 3, 2):
-        d_z[d - 1].wait_recv()
-        total = total + rz[d - 1].astype(F32)
+    total = d_z.result()
     up = total[0:128]
     raw = proj_ref[QPG].astype(F32)
     rk = rsqrt_mean(raw)
@@ -500,8 +601,8 @@
     for copy in p_g:
         copy.wait_recv()
     for q in range(4):
-        gw_ref[q * PIECE : (q + 1) * PIECE, :] = og[q]
-    for copy in sent + p_z + p_l + p_g:
+        gw_ref[q * PIECE : (q + 1) * PIECE, :] = og[q].astype(F32)
+    for copy in sent:
         copy.wait_send()
     for yy in range(4):
 
@@ -521,7 +622,7 @@
             preferred_element_type=F32,
         )
         for r in range(NBR):
-            at = pl.ds(pl.multiple_of(rows_ref[col, r] * BLK, BLK), BLK)
+            at = pl.ds(pl.multiple_of(rows_ref[r, col] * BLK, BLK), BLK)
             piece = spread[:, r * BLK : (r + 1) * BLK]
             if col < NRB // NBR:
                 acc[:, at] = piece
@@ -553,16 +654,17 @@
             shape((NCB, 128, HD)),
             shape((NRB, BLK, 128)),
         ),
-        in_specs=[VM, VM, SM],
+        in_specs=[VM, VM, HB],
         out_specs=(HB, HB, VM, VM),
         scratch_shapes=[
+            pltpu.SMEM((NBR, NCB), jnp.int32),
             pltpu.VMEM((NRB, 128, BLK), BF),
             pltpu.VMEM((2, 4, 4, 4, PIECE, BLK), BF),
             pltpu.VMEM((NCB * NBR * BLK, BLK), BF),
             pltpu.VMEM((2, 4, 4, 256, HD), BF),
-            dma(2), dma(2),
-            dma(3), dma(3), dma(3), dma(3), dma(3, 4), dma(3, 4), dma(4, 4), dma(4, 4),
-            dma(3), dma(3), dma(3, 4), dma(3, 4), dma(4, 4), dma(4, 4),
+            dma(3), dma(2, 4),
+            dma(6), dma(6), dma(3), dma(3), dma(3, 4), dma(3, 4), dma(4, 4), dma(4, 4),
+            dma(6), dma(6), dma(3, 4), dma(3, 4), dma(4, 4), dma(4, 4),
         ],
         compiler_params=pltpu.CompilerParams(
             collective_id=0, has_side_effects=True, vmem_limit_bytes=LIMIT
@@ -576,14 +678,16 @@
     return pl.pallas_call(
         attention_kernel,
         out_shape=(shape((QPG, 128, HD)), shape((32, 256, HD))),
-        in_specs=[SM, VM, VM, VM],
+        in_specs=[HB, HB, VM, VM],
         out_specs=(VM, VM),
         scratch_shapes=[
+            pltpu.SMEM((2, 32), jnp.int32),
+            dma(3),
             pltpu.VMEM((4096, HD), BF),
             pltpu.VMEM((4096, HD), BF),
-            pltpu.VMEM((16, HD, CHUNK), BF),
-            pltpu.VMEM((16, HD, CHUNK), BF),
-            pltpu.VMEM((24, CHUNK, rows), BF),
+            pltpu.VMEM((4096 // CHUNK, HD, CHUNK), BF),
+            pltpu.VMEM((4096 // CHUNK, HD, CHUNK), BF),
+            pltpu.VMEM((6144 // CHUNK, CHUNK, rows), BF),
             pltpu.VMEM((4096, HD), F32),
             pltpu.VMEM((4096, HD), F32),
             pltpu.VMEM((2, rows, HD), BF),
@@ -603,14 +707,19 @@
     return pl.pallas_call(
         reduce_kernel,
         out_shape=(shape((SHARD, BLK), F32), shape((2, 128, HD))),
-        in_specs=[VM, VM, VM, VM, SM],
+        in_specs=[HB, VM, VM, HB, HB],
         out_specs=(VM, VM),
         scratch_shapes=[
+            pltpu.SMEM((NBR, NCB), jnp.int32),
+            pltpu.VMEM((NRB, BLK, 128), BF),
+            pltpu.VMEM((4, 4, 256, HD), BF),
+            dma(6),
             pltpu.VMEM((4, 4, 256, HD), BF),
             pltpu.VMEM((4, 4, 256, HD), BF),
             pltpu.VMEM((3, 4, 256, HD), BF),
             pltpu.VMEM((4, 256, HD), BF),
-            pltpu.VMEM((3, 256, HD), BF),
+            pltpu.VMEM((256, HD), BF),
+            pltpu.VMEM((2, 256, HD), BF),
             pltpu.VMEM((NCB * NBR * BLK, BLK), BF),
             pltpu.VMEM((4, 4, SHARD, BLK), BF),
             pltpu.VMEM((4, 4, 4, PIECE, BLK), BF),
@@ -618,13 +727,13 @@
             pltpu.VMEM((4, 4, PIECE, BLK), BF),
             pltpu.VMEM((3, 4, PIECE, BLK), BF),
             pltpu.VMEM((4, PIECE, BLK), BF),
-            pltpu.VMEM((3, PIECE, BLK), BF),
-            pltpu.VMEM((PIECE, BLK), F32),
-            pltpu.VMEM((3, PIECE, BLK), F32),
-            pltpu.VMEM((4, PIECE, BLK), F32),
-            dma(4), dma(4), dma(3, 4), dma(3, 4), dma(3), dma(3),
+            pltpu.VMEM((PIECE, BLK), BF),
+            pltpu.VMEM((2, PIECE, BLK), BF),
+            pltpu.VMEM((4, PIECE, BLK), BF),
+            pltpu.VMEM((4, PIECE, BLK), BF),
+            dma(4), dma(4), dma(3, 4), dma(3, 4), dma(6), dma(6),
             dma(4, 4), dma(4, 4), dma(3, 4), dma(3, 4), dma(4), dma(3),
-            dma(3), dma(3), dma(3), dma(3), dma(3), dma(3),
+            dma(6), dma(6), dma(3), dma(3), dma(3), dma(3),
         ],
         compiler_params=pltpu.CompilerParams(
             collective_id=1, has_side_effects=True, vmem_limit_bytes=LIMIT
@@ -646,6 +755,7 @@
 
 
 def per_device(tokens, grad_attn, w_packed, block_rows, span_pairs):
+    block_rows, span_pairs = block_rows.T, span_pairs.T
     kv, w_all, proj, tokt = run_forward(tokens[0], w_packed, block_rows)
     gpq, dkv = run_attention(span_pairs, kv.reshape(32, 256, HD), proj, grad_attn[0])
     grad_weights, gpkv = run_reduce(dkv.reshape(2, 4, 4, 256, HD), gpq, proj, tokt, block_rows)

time: 160 us -> 145 us (0.906)
  Pallas kernels: 155 us -> 144 us
  local copies, waits for them, and re-layouts: 3.39 us -> 0.67 us
    pallas_call x1, Pallas kernels: 70.2 us -> 64.9 us  [run_reduce(): pl.pallas_call(reduce_kernel, out_shape=(shape((SHARD, BLK), F32), shape(...]
    pallas_call x1, Pallas kernels: 20.9 us -> 17 us  [run_attention(): pl.pallas_call(attention_kernel, out_shape=(shape((QPG, 128, HD)), shape(...]
    unnamed x5 -> x3, local copies, waits for them, and re-layouts: 3.39 us -> 0.67 us
    pallas_call x1, Pallas kernels: 60.1 us -> 57.8 us  [run_forward(): pl.pallas_call(forward_kernel, out_shape=(shape((2, 4, 4, 256, HD)), shap...]
where the time goes in v2:
time: 145 us
  Pallas kernels  144 us (99%)
    pallas_call x1, Pallas kernels, run_reduce(): pl.pallas_call(reduce_kernel, out_shape=(shape((SHARD, BLK), F32), shape(...  64.9 us
    pallas_call x1, Pallas kernels, run_forward(): pl.pallas_call(forward_kernel, out_shape=(shape((2, 4, 4, 256, HD)), shap...  57.8 us
    pallas_call x1, Pallas kernels, run_attention(): pl.pallas_call(attention_kernel, out_shape=(shape((QPG, 128, HD)), shape(...  17 us
    pallas_call x1, Pallas kernels, run_tokens(): pl.pallas_call(tokens_kernel, out_shape=shape((128, D)), in_specs=[VM, VM...  4.26 us

profile of v2, /device:TPU:24, one launch (start us, length us, event | category | flops | bytes accessed | tf_op | source)
XLA Modules:
  0.0 145.3 jit_solution(15479071861850590342)
XLA Ops:
  0.6 57.8 %forward.1 = (bf16[2,4,4,256,128]{4,3,2,1,0:T(8,128)(2,1)}, bf16[10240,128]{1,0:T(8,128)(2,1)}, bf16[10,128,128]{2,1,0:T(8,128)(2,1)}, bf16[32,128,128]{2,1,0:T(8,128)(2,1)}) custom-call(bf16[128,4096]{1,0:T(8,128)(2,1)} %bitcast.10, bf16[320,128]{1,0:T(8,128)(2,1)} %w_ref.1, s32[8,10]{1,0:T(8,128)} %bitcast.12), custom_call_target="tpu_custom_call" | custom-call | tf_op jit(solution)/shard_map/forward/pallas_call | solution.py:649
  58.4 17.0 %attention.1 = (bf16[8,128,128]{2,1,0:T(8,128)(2,1)}, bf16[32,256,128]{2,1,0:T(8,128)(2,1)}) custom-call(s32[2,32]{1,0:T(2,128)} %bitcast.15, bf16[32,256,128]{2,1,0:T(8,128)(2,1)} %bitcast.7, bf16[10,128,128]{2,1,0:T(8,128)(2,1)} %get-tuple-element.11.proj_ref, bf16[128,1024]{1,0:T(8,128)(2,1)} %bitcast.11), custom_call_target="tpu_custom_call" | custom-call | tf_op jit(solution)/shard_map/attention/pallas_call | solution.py:678
  75.5 64.9 %reduce.1 = (f32[320,128]{1,0:T(8,128)}, bf16[2,128,128]{2,1,0:T(8,128)(2,1)}) custom-call(bf16[2,4,4,256,128]{4,3,2,1,0:T(8,128)(2,1)} %bitcast.8, bf16[8,128,128]{2,1,0:T(8,128)(2,1)} %get-tuple-element.12.gpq_ref, bf16[10,128,128]{2,1,0:T(8,128)(2,1)} %get-tuple-element.11.proj_ref, bf16[32,128,128]{2,1,0:T(8,128)(2,1)} %get-tuple-element.14.tokens_ref, ...), custom_call_target="tpu_custom_call" | custom-call | tf_op jit(solution)/shard_map/reduce/pallas_call | solution.py:707
  140.4 0.0 copy-start
  140.4 4.3 %tokens.1 = bf16[128,4096]{1,0:T(8,128)(2,1)} custom-call(bf16[8,128,128]{2,1,0:T(8,128)(2,1)} %get-tuple-element.12.gpq_ref, bf16[2,128,128]{2,1,0:T(8,128)(2,1)} %get-tuple-element.15.gpkv_ref, bf16[10240,128]{1,0:T(8,128)(2,1)} %get-tuple-element.16.w_ref, s32[8,10]{1,0:T(8,128)} %bitcast.14), custom_call_target="tpu_custom_call" | custom-call | tf_op jit(solution)/shard_map/tokens/pallas_call | solution.py:746
  144.7 0.0 copy-done
  144.7 0.7 copy.8
Async XLA Ops:
  140.4 4.3 %copy-start = (f32[320,128]{1,0:T(8,128)S(1)}, f32[320,128]{1,0:T(8,128)}, u32[]{:S(2)}) copy-start(f32[320,128]{1,0:T(8,128)} %get-tuple-element.21) | copy-start | bytes 491524

commit v3 on v2

--- a/solution.py
+++ b/solution.py
@@ -123,14 +123,18 @@
 
 
 def forward_kernel(
-    tok_ref, w_ref, table_ref, kv_out, w_out, proj_ref, tokt_ref,
-    rows_ref, tokb, wb, wall, kvb, loc, outs,
-    wzs, wzr, wys, wyr, wxs, wxr, wcs, wcr, kzs, kzr, kys, kyr, kcs, kcr,
+    tok_ref, w_ref, table_ref, kv_out, w_out, proj_ref, tokt_out,
+    rows_ref, tokb, turned, wb, wall, kvb, loc, outs,
+    wzs, wzr, wys, wyr, wxs, wxr, wcs, wcr, uys, uyr, uxs, uxr, ucs, ucr, kzs, kzr, kys, kyr, kcs, kcr,
 ):
     x, l, y, h, c = place()
     to = peers()
     table = pltpu.make_async_copy(table_ref, rows_ref, loc.at[2])
     table.start()
+    for b in range(NRB):
+        pltpu.make_async_copy(
+            tok_ref.at[:, b * BLK : (b + 1) * BLK], tokb.at[b], loc.at[3]
+        ).start()
     enter(
         [to[a](d) for a in ("y", "x") for d in (1, 2, 3)] + [to["h"](1), to["h"](3), to["c"](1)]
     )
@@ -161,28 +165,62 @@
     )
     for copy in wz.own:
         go(copy)
+    pltpu.make_async_copy(tokb, tokb, loc.at[3]).wait()
     for b in range(NRB):
-        tokb[b] = tok_ref[:, b * BLK : (b + 1) * BLK]
-        tokt_ref[b] = tok_ref[:, b * BLK : (b + 1) * BLK].T
-    mine.wait()
-    for index in range(2):
-        wz.own[index].wait_recv()
-        go(wz.relay[index])
-    for copy in wz.own[2:] + wz.relay:
-        copy.wait_recv()
+        turned[b] = tokb[b].T
+    def u_y(d, hh):
+        piece = wb.at[c, x, 3, hh]
+        return remote(piece, piece, uys.at[d - 1, hh], uyr.at[d - 1, hh], to["y"](d))
+
+    def u_x(d, hh):
+        piece = wb.at[c, x, 3, hh]
+        return remote(piece, piece, uxs.at[d - 1, hh], uxr.at[d - 1, hh], to["x"](d))
+
+    def u_c(xx, hh):
+        piece = wb.at[c, xx, 3, hh]
+        return remote(piece, piece, ucs.at[xx, hh], ucr.at[xx, hh], to["c"](1))
+
+    for step in (0, 1, 3, 2):
+        hh = (h + 4 - step) % 4
+        if step == 0:
+            mine.wait()
+        elif step == 1:
+            for index in range(2):
+                wz.own[index].wait_recv()
+                go(wz.relay[index])
+            wz.own[2].wait_recv()
+        elif step == 3:
+            wz.own[3].wait_recv()
+        else:
+            for copy in wz.relay:
+                copy.wait_recv()
+
+        @pl.when(y == 3)
+        def _():
+            for d in (2, 1, 3):
+                u_y(d, hh).start()
+
+        @pl.when(y != 3)
+        def _():
+            remote(
+                wb.at[c, x, 3, hh], wb.at[c, x, 3, hh], uys.at[y, hh], uyr.at[y, hh], to["y"](1)
+            ).wait_recv()
+
+        for d in (2, 1, 3):
+            go(u_x(d, hh))
+        go(u_c(x, hh))
+
     ys = [
         remote(wb.at[c, x, y], wb.at[c, x, y], wys.at[d - 1], wyr.at[d - 1], to["y"](d))
         for d in (2, 1, 3)
     ]
-    sent.extend(ys)
-
-    @pl.when(y == 3)
+
+    @pl.when(y != 3)
     def _():
         for copy in ys:
             copy.start()
 
-    for yy in (3, 0, 1, 2):
-
+    def take_y(yy):
         @pl.when(y != yy)
         def _():
             back = (y + 3 - yy) % 4
@@ -193,12 +231,6 @@
         for d in (2, 1, 3):
             go(w_x(d, yy))
         go(w_c(x, yy))
-        if yy == 3:
-
-            @pl.when(y != 3)
-            def _():
-                for copy in ys:
-                    copy.start()
 
     def forward_x(yy):
         for d in (1, 3, 2):
@@ -207,7 +239,11 @@
 
     def assemble(yy):
         for xx in range(4):
-            w_c(xx, yy).wait_recv()
+            if yy == 3:
+                for hh in range(4):
+                    u_c(xx, hh).wait_recv()
+            else:
+                w_c(xx, yy).wait_recv()
         for cc in range(2):
             for hh in range(4):
                 for q in range(4):
@@ -223,7 +259,13 @@
             chosen, wall[col * rows : (col + 1) * rows, :], preferred_element_type=F32
         ).astype(BF)
 
-    forward_x(3)
+    save_t = pltpu.make_async_copy(turned, tokt_out, loc.at[4])
+    save_t.start()
+    for step in (0, 1, 3, 2):
+        hh = (h + 4 - step) % 4
+        for d in (1, 3, 2):
+            u_x(d, hh).wait_recv()
+            go(u_c((x + 4 - d) % 4, hh))
     table.wait()
     assemble(3)
     key = project(QPG)
@@ -255,7 +297,7 @@
         go(k_y(d, h))
     go(k_c(y, h))
     for yy in (0, 1, 2):
-        forward_x(yy)
+        take_y(yy)
     for index in range(2):
         kz.own[index].wait_recv()
         go(kz.relay[index])
@@ -267,16 +309,23 @@
             go(k_y(e, hh))
         go(k_c(y, hh))
     for yy in (0, 1, 2):
+        forward_x(yy)
+
+    def forward_k(step):
+        hh = (h + 4 - step) % 4
+        for d in (1, 3, 2):
+            k_y(d, hh).wait_recv()
+            go(k_c((y + 4 - d) % 4, hh))
+
+    for step in (0, 1, 3):
+        forward_k(step)
+    for yy in (0, 1, 2):
         assemble(yy)
     save_w = pltpu.make_async_copy(wall, w_out, loc.at[1])
     save_w.start()
     for col in range(QPG):
         proj_ref[col] = project(col)
-    for step in (0, 1, 3, 2):
-        hh = (h + 4 - step) % 4
-        for d in (1, 3, 2):
-            k_y(d, hh).wait_recv()
-            go(k_c((y + 4 - d) % 4, hh))
+    forward_k(2)
     saves = []
     for step in (0, 1, 3, 2):
         hh = (h + 4 - step) % 4
@@ -288,9 +337,22 @@
             saves.append(save)
     for copy in sent:
         copy.wait_send()
+
+    @pl.when(y != 3)
+    def _():
+        for copy in ys:
+            copy.wait_send()
+
+    @pl.when(y == 3)
+    def _():
+        for hh in range(4):
+            for d in (1, 2, 3):
+                u_y(d, hh).wait_send()
+
     for save in saves:
         save.wait()
     save_w.wait()
+    save_t.wait()
 
 
 def attention_kernel(
@@ -419,30 +481,34 @@
 
     lax.fori_loop(chunks(1), 4096 // CHUNK, clear, 0)
 
-    def scatter(owner, _):
-        spot = (owner % 2) * 16 + owner // 2
-        for part in range(2):
-            at = pl.multiple_of(pairs_ref[part, owner] * SPAN, SPAN)
-            low = part * SPAN
-            dkv_ref[spot, low : low + SPAN, :] = dk[pl.ds(at, SPAN), :].astype(BF)
-            dkv_ref[spot, 128 + low : 128 + low + SPAN, :] = (
-                dv[pl.ds(at, SPAN), :] * math.sqrt(HD)
-            ).astype(BF)
+    def scatter(block, _):
+        for step in range(4):
+            owner = block * 4 + step
+            spot = (step % 2) * 16 + block * 2 + step // 2
+            for part in range(2):
+                at = pl.ds(pl.multiple_of(pairs_ref[part, owner] * SPAN, SPAN), SPAN)
+                low = part * SPAN
+                dkv_ref[spot, low : low + SPAN, :] = dk[at, :].astype(BF)
+                dkv_ref[spot, 128 + low : 128 + low + SPAN, :] = (
+                    dv[at, :] * math.sqrt(HD)
+                ).astype(BF)
         return 0
 
-    lax.fori_loop(0, 32, scatter, 0)
+    lax.fori_loop(0, 8, scatter, 0)
 
 
 def reduce_kernel(
     dkv_ref, gpq_ref, proj_ref, tokens_ref, table_ref, gw_ref, gpkv_ref,
     rows_ref, tokt_ref, dl, loc, rc, sb, ry, s2, rf, rz, pw, wc, sx, rx, ty, wy, tz, wf, wz, lb, og,
-    dcs, dcr, dys, dyr, dzs, dzr, pcs, pcr, pxs, pxr, pys, pyr, pzs, pzr, pls, plr, pgs, pgr,
+    dcs, dcr, dys, dyr, dzs, dzr, pcs, pcr, pxs, pxr, pys, pyr, vxs, vxr, vys, vyr, pzs, pzr, pls, plr, pgs, pgr,
 ):
     x, l, y, h, c = place()
     to = peers()
     table = pltpu.make_async_copy(table_ref, rows_ref, loc.at[4])
     turned = pltpu.make_async_copy(tokens_ref, tokt_ref, loc.at[5])
-    loads = [pltpu.make_async_copy(dkv_ref.at[c, yy], dl.at[yy], loc.at[yy]) for yy in range(4)]
+    loads = [
+        pltpu.make_async_copy(dkv_ref.at[c, :, hh], dl.at[:, hh], loc.at[hh]) for hh in range(4)
+    ]
     for copy in loads + [table, turned]:
         copy.start()
     enter(
@@ -455,11 +521,13 @@
         copy.start()
         sent.append(copy)
 
-    def d_c(yy):
-        return remote(dkv_ref.at[1 - c, yy], rc.at[yy], dcs.at[yy], dcr.at[yy], to["c"](1))
-
-    for d in (2, 1, 3, 0):
-        go(d_c((y + d) % 4))
+    def d_c(hh):
+        return remote(
+            dkv_ref.at[1 - c, :, hh], rc.at[:, hh], dcs.at[hh], dcr.at[hh], to["c"](1)
+        )
+
+    for step in (2, 1, 3, 0):
+        go(d_c((h + step) % 4))
 
     def partial(col, grad):
         chosen = jnp.concatenate([tokt_ref[rows_ref[r, col]] for r in range(NBR)], axis=0)
@@ -475,11 +543,11 @@
 
     for copy in loads:
         copy.wait()
-    for d in (2, 1, 3, 0):
-        yy = (y + d) % 4
-        d_c(yy).wait_recv()
-        for step in (2, 1, 3, 0):
-            hh = (h + step) % 4
+    for step in (2, 1, 3, 0):
+        hh = (h + step) % 4
+        d_c(hh).wait_recv()
+        for d in (2, 1, 3, 0):
+            yy = (y + d) % 4
             sb[yy, hh] = (dl[yy, hh].astype(F32) + rc[yy, hh].astype(F32)).astype(BF)
             if d:
                 go(d_y(d, hh))
@@ -515,24 +583,43 @@
                 go(copy)
         elif step:
             go(d_z.direct[step // 2])
-    d_z.pass_on(go)
 
     def p_x(d, yy):
         return remote(
             sx.at[(x + d) % 4, yy], rx.at[d - 1, yy], pxs.at[d - 1, yy], pxr.at[d - 1, yy], to["x"](d)
         )
 
+    def fold_piece(yy, hh):
+        p_c(yy, hh).wait_recv()
+        row = pl.multiple_of(((yy * 4 + hh) * 2 + c) * SHARD, 64)
+        for q in range(4):
+            sx[q, yy, hh] = (
+                pw[pl.ds(row + q * PIECE, PIECE), :].astype(F32)
+                + wc[yy, hh, q * PIECE : (q + 1) * PIECE, :].astype(F32)
+            ).astype(BF)
+
     def fold_core(yy):
         for hh in range(4):
-            p_c(yy, hh).wait_recv()
-            row = pl.multiple_of(((yy * 4 + hh) * 2 + c) * SHARD, 64)
-            for q in range(4):
-                sx[q, yy, hh] = (
-                    pw[pl.ds(row + q * PIECE, PIECE), :].astype(F32)
-                    + wc[yy, hh, q * PIECE : (q + 1) * PIECE, :].astype(F32)
-                ).astype(BF)
+            fold_piece(yy, hh)
         for d in (2, 1, 3):
             go(p_x(d, yy))
+
+    def v_x(d, hh):
+        return remote(
+            sx.at[(x + d) % 4, 3, hh],
+            rx.at[d - 1, 3, hh],
+            vxs.at[d - 1, hh],
+            vxr.at[d - 1, hh],
+            to["x"](d),
+        )
+
+    def v_y(hh):
+        d = (2 - y) % 4
+        return remote(
+            ty.at[3, hh], wy.at[d, hh], vys.at[hh], vyr.at[d, hh], (l * 4 + x, 24 + h * 2 + c)
+        )
+
+    order = [(h + step) % 4 for step in (2, 1, 3, 0)]
 
     def p_y(yy):
         d = (yy + 3 - y) % 4
@@ -558,13 +645,32 @@
     ]
 
     def finish():
-        total = ty[y].astype(F32)
-        for d in (1, 3, 2):
-            remote(ty.at[0], wy.at[d - 1], pys.at[0], pyr.at[d - 1], to["y"](1)).wait_recv()
-            total = total + wy[d - 1].astype(F32)
-        tz[...] = total.astype(BF)
-        for copy in p_z.first + p_z.direct:
-            go(copy)
+        starts = p_z.first + p_z.direct
+
+        @pl.when(y != 3)
+        def _():
+            total = ty[y].astype(F32)
+            for d in (1, 3, 2):
+                remote(ty.at[0], wy.at[d - 1], pys.at[0], pyr.at[d - 1], to["y"](1)).wait_recv()
+                total = total + wy[d - 1].astype(F32)
+            tz[...] = total.astype(BF)
+            for copy in starts:
+                copy.start()
+
+        @pl.when(y == 3)
+        def _():
+            for index, hh in enumerate(order):
+                total = ty[3, hh].astype(F32)
+                for d in (1, 3, 2):
+                    remote(
+                        ty.at[0, 0], wy.at[d - 1, hh], vys.at[0], vyr.at[d - 1, hh], to["y"](1)
+                    ).wait_recv()
+                    total = total + wy[d - 1, hh].astype(F32)
+                tz[hh] = total.astype(BF)
+                for copy in (starts[:2], starts[2:3], starts[3:], [])[index]:
+                    copy.start()
+
+        sent.extend(starts)
         p_z.pass_on(go)
         lb[l] = p_z.result().astype(BF)
         for d in (2, 1, 3):
@@ -577,6 +683,7 @@
         for d in (2, 1, 3):
             go(p_g[d - 1])
 
+    d_z.pass_on(go)
     for yy in (0, 1, 2):
         fold_core(yy)
     total = d_z.result()
@@ -591,27 +698,46 @@
     gpkv_ref[1] = grad_value
     partial(QPG, grad_key)
     partial(QPG + 1, grad_value)
-    for hh in range(4):
+    for hh in order:
         go(p_c(3, hh))
+    for hh in order:
+        fold_piece(3, hh)
+        for d in (2, 1, 3):
+            go(v_x(d, hh))
     for yy in (0, 1, 2):
         fold_x(yy)
-    fold_core(3)
-    fold_x(3)
+    for hh in order:
+        total = sx[x, 3, hh].astype(F32)
+        for d in (1, 3, 2):
+            v_x(d, hh).wait_recv()
+            total = total + rx[d - 1, 3, hh].astype(F32)
+        ty[3, hh] = total.astype(BF)
+
+        @pl.when(y != 3)
+        def _():
+            v_y(hh).start()
+
     finish()
     for copy in p_g:
         copy.wait_recv()
     for q in range(4):
-        gw_ref[q * PIECE : (q + 1) * PIECE, :] = og[q].astype(F32)
+        gw_ref[q * PIECE : (q + 1) * PIECE, :] = og[q]
     for copy in sent:
         copy.wait_send()
-    for yy in range(4):
+    for yy in range(3):
 
         @pl.when(y != yy)
         def _():
             p_y(yy).wait_send()
 
-
-def tokens_kernel(gpq_ref, gpkv_ref, w_ref, rows_ref, out_ref, acc):
+    @pl.when(y != 3)
+    def _():
+        for hh in range(4):
+            v_y(hh).wait_send()
+
+
+def tokens_kernel(gpq_ref, gpkv_ref, w_ref, gw_ref, rows_ref, out_ref, weights_ref, acc):
+    weights_ref[...] = gw_ref[...].astype(F32)
     rows = NBR * BLK
     for col in range(NCB):
         grad = gpq_ref[col] if col < QPG else gpkv_ref[col - QPG]
@@ -654,16 +780,18 @@
             shape((NCB, 128, HD)),
             shape((NRB, BLK, 128)),
         ),
-        in_specs=[VM, VM, HB],
-        out_specs=(HB, HB, VM, VM),
+        in_specs=[HB, VM, HB],
+        out_specs=(HB, HB, VM, HB),
         scratch_shapes=[
             pltpu.SMEM((NBR, NCB), jnp.int32),
             pltpu.VMEM((NRB, 128, BLK), BF),
+            pltpu.VMEM((NRB, BLK, 128), BF),
             pltpu.VMEM((2, 4, 4, 4, PIECE, BLK), BF),
             pltpu.VMEM((NCB * NBR * BLK, BLK), BF),
             pltpu.VMEM((2, 4, 4, 256, HD), BF),
-            dma(3), dma(2, 4),
-            dma(6), dma(6), dma(3), dma(3), dma(3, 4), dma(3, 4), dma(4, 4), dma(4, 4),
+            dma(5), dma(2, 4),
+            dma(6), dma(6), dma(3), dma(3), dma(3, 3), dma(3, 3), dma(4, 3), dma(4, 3),
+            dma(3, 4), dma(3, 4), dma(3, 4), dma(3, 4), dma(4, 4), dma(4, 4),
             dma(6), dma(6), dma(3, 4), dma(3, 4), dma(4, 4), dma(4, 4),
         ],
         compiler_params=pltpu.CompilerParams(
@@ -706,7 +834,7 @@
 def run_reduce(dkv, gpq, proj, tokt, block_rows):
     return pl.pallas_call(
         reduce_kernel,
-        out_shape=(shape((SHARD, BLK), F32), shape((2, 128, HD))),
+        out_shape=(shape((SHARD, BLK)), shape((2, 128, HD))),
         in_specs=[HB, VM, VM, HB, HB],
         out_specs=(VM, VM),
         scratch_shapes=[
@@ -732,7 +860,8 @@
             pltpu.VMEM((4, PIECE, BLK), BF),
             pltpu.VMEM((4, PIECE, BLK), BF),
             dma(4), dma(4), dma(3, 4), dma(3, 4), dma(6), dma(6),
-            dma(4, 4), dma(4, 4), dma(3, 4), dma(3, 4), dma(4), dma(3),
+            dma(4, 4), dma(4, 4), dma(3, 3), dma(3, 3), dma(3), dma(3),
+            dma(3, 4), dma(3, 4), dma(4), dma(3, 4),
             dma(6), dma(6), dma(3), dma(3), dma(3), dma(3),
         ],
         compiler_params=pltpu.CompilerParams(
@@ -742,24 +871,24 @@
     )(dkv, gpq, proj, tokt, block_rows)
 
 
-def run_tokens(gpq, gpkv, w_all, block_rows):
+def run_tokens(gpq, gpkv, w_all, sums, block_rows):
     return pl.pallas_call(
         tokens_kernel,
-        out_shape=shape((128, D)),
-        in_specs=[VM, VM, VM, SM],
-        out_specs=VM,
+        out_shape=(shape((128, D)), shape((SHARD, BLK), F32)),
+        in_specs=[VM, VM, VM, VM, SM],
+        out_specs=(VM, VM),
         scratch_shapes=[pltpu.VMEM((128, D), F32)],
         compiler_params=pltpu.CompilerParams(vmem_limit_bytes=LIMIT),
         name="tokens",
-    )(gpq, gpkv, w_all, block_rows)
+    )(gpq, gpkv, w_all, sums, block_rows)
 
 
 def per_device(tokens, grad_attn, w_packed, block_rows, span_pairs):
     block_rows, span_pairs = block_rows.T, span_pairs.T
     kv, w_all, proj, tokt = run_forward(tokens[0], w_packed, block_rows)
     gpq, dkv = run_attention(span_pairs, kv.reshape(32, 256, HD), proj, grad_attn[0])
-    grad_weights, gpkv = run_reduce(dkv.reshape(2, 4, 4, 256, HD), gpq, proj, tokt, block_rows)
-    grad_tokens = run_tokens(gpq, gpkv, w_all, block_rows)
+    sums, gpkv = run_reduce(dkv.reshape(2, 4, 4, 256, HD), gpq, proj, tokt, block_rows)
+    grad_tokens, grad_weights = run_tokens(gpq, gpkv, w_all, sums, block_rows)
     return (grad_tokens[None], grad_weights)
 
 

time: 145 us -> 134 us (0.924)
  Pallas kernels: 144 us -> 133 us
    pallas_call x2, Pallas kernels: 69.2 us -> 62.4 us  [the longest x1 58.1 us: run_reduce(): pl.pallas_call(reduce_kernel, out_shape=(shape((SHARD, BLK)), shape((2, 1...]
    pallas_call x1, Pallas kernels: 57.8 us -> 54.2 us  [run_forward(): pl.pallas_call(forward_kernel, out_shape=(shape((2, 4, 4, 256, HD)), shap...]
where the time goes in v3:
time: 134 us
  Pallas kernels  133 us (99%)
    pallas_call x1, Pallas kernels, run_reduce(): pl.pallas_call(reduce_kernel, out_shape=(shape((SHARD, BLK)), shape((2, 1...  58.1 us
    pallas_call x1, Pallas kernels, run_forward(): pl.pallas_call(forward_kernel, out_shape=(shape((2, 4, 4, 256, HD)), shap...  54.2 us
    pallas_call x1, Pallas kernels, run_attention(): pl.pallas_call(attention_kernel, out_shape=(shape((QPG, 128, HD)), shape(...  16.5 us
    pallas_call x1, Pallas kernels, run_tokens(): pl.pallas_call(tokens_kernel, out_shape=(shape((128, D)), shape((SHARD, B...  4.26 us

profile of v3, /device:TPU:24, one launch (start us, length us, event | category | flops | bytes accessed | tf_op | source)
XLA Modules:
  0.0 133.6 jit_solution(18315696903239330887)
XLA Ops:
  0.6 54.2 %forward.1 = (bf16[2,4,4,256,128]{4,3,2,1,0:T(8,128)(2,1)}, bf16[10240,128]{1,0:T(8,128)(2,1)}, bf16[10,128,128]{2,1,0:T(8,128)(2,1)}, bf16[32,128,128]{2,1,0:T(8,128)(2,1)}) custom-call(bf16[128,4096]{1,0:T(8,128)(2,1)} %bitcast.9, bf16[320,128]{1,0:T(8,128)(2,1)} %w_ref.1, s32[8,10]{1,0:T(8,128)} %bitcast.11), custom_call_target="tpu_custom_call" | custom-call | tf_op jit(solution)/shard_map/forward/pallas_call | solution.py:775
  54.8 16.5 %attention.1 = (bf16[8,128,128]{2,1,0:T(8,128)(2,1)}, bf16[32,256,128]{2,1,0:T(8,128)(2,1)}) custom-call(s32[2,32]{1,0:T(2,128)} %bitcast.14, bf16[32,256,128]{2,1,0:T(8,128)(2,1)} %bitcast.7, bf16[10,128,128]{2,1,0:T(8,128)(2,1)} %get-tuple-element.13.proj_ref, bf16[128,1024]{1,0:T(8,128)(2,1)} %bitcast.10), custom_call_target="tpu_custom_call" | custom-call | tf_op jit(solution)/shard_map/attention/pallas_call | solution.py:806
  71.3 58.1 %reduce.1 = (bf16[320,128]{1,0:T(8,128)(2,1)}, bf16[2,128,128]{2,1,0:T(8,128)(2,1)}) custom-call(bf16[2,4,4,256,128]{4,3,2,1,0:T(8,128)(2,1)} %bitcast.8, bf16[8,128,128]{2,1,0:T(8,128)(2,1)} %get-tuple-element.14.gpq_ref, bf16[10,128,128]{2,1,0:T(8,128)(2,1)} %get-tuple-element.13.proj_ref, bf16[32,128,128]{2,1,0:T(8,128)(2,1)} %get-tuple-element.16.tokens_ref, ...), custom_call_target="tpu_custom_call" | custom-call | tf_op jit(solution)/shard_map/reduce/pallas_call | solution.py:835
  129.4 4.3 %tokens.1 = (bf16[128,4096]{1,0:T(8,128)(2,1)}, f32[320,128]{1,0:T(8,128)}) custom-call(bf16[8,128,128]{2,1,0:T(8,128)(2,1)} %get-tuple-element.14.gpq_ref, bf16[2,128,128]{2,1,0:T(8,128)(2,1)} %get-tuple-element.17.gpkv_ref, bf16[10240,128]{1,0:T(8,128)(2,1)} %get-tuple-element.18.w_ref, bf16[320,128]{1,0:T(8,128)(2,1)} %get-tuple-element.19.gw_ref, ...), custom_call_target="tpu_custom_call" | custom-call | tf_op jit(solution)/shard_map/tokens/pallas_call | solution.py:875
